TPU v7x, 128 devices: a whole 4x4x4 slice. The times are simulated.
128 devices in a mesh: seq: 4 (over y), exp: 32 (over z, x, core).
Axes of the slice: x: 4, y: 4, z: 4, core: 2. Of those that a mesh axis runs over, the one named last changes fastest.
Arguments:
- queries: bfloat16 [32, 512, 4096], P('exp', 'seq'), may hold values from -36 to 36
- rotated_keys: bfloat16 [32, 512, 512], P('exp', 'seq'), may hold values from -4 to 4
- projected_values: bfloat16 [32, 512, 512], P('exp', 'seq'), may hold values from -4 to 4
- doc_ids: int32 [32, 512], P('exp'), may hold values from 0 to 3, never falling along the last dimension, each value on 1 to 256 neighbouring positions
- residual: bfloat16 [32, 512, 4096], P('exp', 'seq'), may hold values from -14 to 14
- out_weight: bfloat16 [4096, 4096], P('seq', 'exp'), may hold values from -0.09375 to 0.09375
- norm_gain: float32 [4096], replicated, may hold values from 0.1 to 1.9
- routes: int32 [32, 512, 8], P('exp', 'seq'), may hold values from 0 to 127, as said below
- gate_vals: float32 [32, 512, 8], P('exp', 'seq'), may hold values from 0.05 to 0.35
- cotangent: bfloat16 [32, 512, 4096], P('exp', 'seq'), may hold values from -0.119628906 to 0.119628906
- expert_in: bfloat16 [128, 4096, 1536], P(('seq', 'exp')), may hold values from -0.09375 to 0.09375
- expert_down: bfloat16 [128, 768, 4096], P(('seq', 'exp')), may hold values from -0.21875 to 0.21875
Outputs:
- layer_out: bfloat16 [32, 512, 4096], P('exp', 'seq')
- gate_grad: float32 [32, 512, 8], P('exp', 'seq')
Inputs may be any that keep to these rules, and one draw needn't show every extreme that they name: `routes`: each token names 8 different experts; the tokens of one device name no expert more than 10 times, and one expert, the same for all devices, exactly 10 times on every device. `doc_ids`: document numbers never fall along a pack; a document holds at most 256 positions.
All inputs are finite; a program needn't handle non-finite values.
Results may differ from a plain program's by a relative error of at most 0.0067.
Values may be sent and summed in bfloat16 or wider, within the bound.
No kernel may reach another device: no remote copies, remote signals or barrier semaphores. Data moves between devices by JAX's collectives and lax.ppermute only.
A program may use at most 192 MiB of HBM per device.

v0:
```python
import math

import jax
import jax.numpy as jnp
from jax import lax
from jax.sharding import PartitionSpec as P

QUERY_HEADS = 32
KEY_VALUE_HEADS = 4
HEAD_SIZE = 128


def sent_together(arrays, axis, split_dim, concat_dim, along):
    ends, at = ([], 0)
    for a in arrays[:-1]:
        at += a.shape[along]
        ends.append(at)
    both = jnp.concatenate(arrays, axis=along)
    return tuple(
        jnp.split(
            lax.all_to_all(both, axis, split_axis=split_dim, concat_axis=concat_dim, tiled=True),
            ends,
            axis=along,
        )
    )


def in_blocks(array, dim, size):
    lengths = array.shape
    parts = array.reshape(*lengths[:dim], size, lengths[dim] // size, *lengths[dim + 1 :])
    return jnp.moveaxis(parts, dim, 0)


def piece_ends(length, count):
    unit = 8 if length >= 8 * count else 1
    return [length // unit * k // count * unit for k in range(1, count)]


def laid_out(parts, dim):
    parts = jnp.moveaxis(parts, 0, dim)
    lengths = parts.shape
    return parts.reshape(*lengths[:dim], lengths[dim] * lengths[dim + 1], *lengths[dim + 2 :])


def several_exchanges(array, axis, pieces, split_dim, concat_dim):
    parts = in_blocks(array, split_dim, lax.axis_size(axis))
    cut = max(range(1, max(2, parts.ndim - 1)), key=lambda d: parts.shape[d])
    done = []
    for piece in jnp.split(parts, piece_ends(parts.shape[cut], pieces), axis=cut):
        if piece.size:
            done.append(lax.all_to_all(piece, axis, split_axis=0, concat_axis=0, tiled=True))
    return laid_out(jnp.concatenate(done, axis=cut), concat_dim)


def attend_heads(q_heads, k_heads, v_heads, doc_rows):
    length = q_heads.shape[0]
    grouping_factor = QUERY_HEADS // KEY_VALUE_HEADS
    block_rows = math.gcd(length, 512)
    block_count = length // block_rows
    score_scale = 1.0 / math.sqrt(HEAD_SIZE)
    positions = jnp.arange(length)
    starts = jnp.arange(block_count, dtype=jnp.int32) * block_rows
    key_rows = k_heads
    value_rows = v_heads
    query_rows = q_heads
    query_rows = query_rows.reshape(block_count, block_rows, grouping_factor, HEAD_SIZE)

    def attend_block(inputs, key_rows=key_rows, value_rows=value_rows):
        query_block, start = inputs
        row_ids = start + jnp.arange(block_rows)
        allowed = (positions[None, :] <= row_ids[:, None]) & (
            doc_rows[None, :] == doc_rows[:, None]
        )
        scores = (
            jnp.einsum("rgd,jd->grj", query_block, key_rows, preferred_element_type=jnp.float32)
            * score_scale
        )
        scores = jnp.where(allowed[None], scores, -jnp.inf)
        row_max = jnp.max(scores, axis=-1, keepdims=True)
        raised = jnp.exp(scores - row_max)
        weights_bf = (raised / jnp.sum(raised, axis=-1, keepdims=True)).astype(jnp.bfloat16)
        block_out = jnp.einsum(
            "grj,jd->rgd", weights_bf, value_rows, preferred_element_type=jnp.float32
        )
        return block_out.astype(jnp.bfloat16).reshape(block_rows, grouping_factor * HEAD_SIZE)

    pieces = lax.map(attend_block, (query_rows, starts)).reshape(
        length, grouping_factor * HEAD_SIZE
    )
    return pieces


def shards(
    queries,
    rotated_keys,
    projected_values,
    doc_ids,
    residual,
    out_weight,
    norm_gain,
    routes,
    gate_vals,
    cotangent,
    expert_in,
    expert_down,
):
    seq_count = lax.axis_size("seq")
    exp_count = lax.axis_size("exp")
    experts = seq_count * exp_count
    token_count = queries.shape[1]
    top_count = routes.shape[2]
    model_width = residual.shape[2]
    hidden = expert_in.shape[2] // 2
    pair_count = token_count * top_count
    capacity = max(2, 5 * pair_count // (4 * experts))
    slot_limit = experts * capacity
    q_heads, k_heads, v_heads = (
        lax.all_to_all(queries, "seq", split_axis=2, concat_axis=1, tiled=True),
        *sent_together((rotated_keys, projected_values), "seq", 2, 1, 0),
    )
    attended = attend_heads(q_heads[0], k_heads[0], v_heads[0], doc_ids[0])
    full_rows = lax.all_gather(out_weight, "exp", axis=1, tiled=True)
    projected = lax.psum_scatter(
        jnp.dot(attended, full_rows, preferred_element_type=jnp.float32),
        "seq",
        scatter_dimension=0,
        tiled=True,
    )
    hidden_state = residual[0].astype(jnp.float32) + projected
    root_mean = jnp.sqrt(jnp.mean(hidden_state * hidden_state, axis=-1, keepdims=True) + 1e-06)
    normed = (hidden_state / root_mean * norm_gain).astype(jnp.bfloat16)
    chosen = routes[0].reshape(pair_count)
    one_hot = (chosen[:, None] == jnp.arange(experts, dtype=jnp.int32)[None, :]).astype(jnp.int32)
    before = jnp.cumsum(one_hot, axis=0) - one_hot
    slot_index = jnp.sum(before * one_hot, axis=1)
    target = chosen * capacity + slot_index
    sources = jnp.repeat(normed, top_count, axis=0)
    outgoing = jnp.zeros((slot_limit, model_width), jnp.bfloat16).at[target].set(sources)
    incoming = lax.all_to_all(
        outgoing.reshape(experts, capacity, model_width),
        ("seq", "exp"),
        split_axis=0,
        concat_axis=0,
        tiled=True,
    )
    incoming = incoming.reshape(slot_limit, model_width)
    weight_in = expert_in[0]
    weight_down = expert_down[0]
    gate_up = jnp.dot(incoming, weight_in, preferred_element_type=jnp.float32)
    activated = (jax.nn.silu(gate_up[:, :hidden]) * gate_up[:, hidden:]).astype(jnp.bfloat16)
    results = jnp.dot(activated, weight_down, preferred_element_type=jnp.float32).astype(
        jnp.bfloat16
    )
    returned = several_exchanges(
        results.reshape(experts, capacity, model_width), ("seq", "exp"), 2, 0, 0
    )
    returned = returned.reshape(slot_limit, model_width)
    picked = returned[target].reshape(token_count, top_count, model_width)
    weights = gate_vals[0]
    mixed = hidden_state + jnp.sum(weights[:, :, None] * picked.astype(jnp.float32), axis=1)
    layer_out = mixed.astype(jnp.bfloat16)[None]
    gate_grad = jnp.einsum("tkd,td->tk", picked, cotangent[0], preferred_element_type=jnp.float32)[
        None
    ]
    return (layer_out, gate_grad)


def solution(mesh):
    in_specs = (
        P("exp", "seq", None),
        P("exp", "seq", None),
        P("exp", "seq", None),
        P("exp", None),
        P("exp", "seq", None),
        P("seq", "exp"),
        P(),
        P("exp", "seq", None),
        P("exp", "seq", None),
        P("exp", "seq", None),
        P(("seq", "exp"), None, None),
        P(("seq", "exp"), None, None),
    )
    out_specs = (P("exp", "seq", None), P("exp", "seq", None))
    return jax.shard_map(shards, mesh=mesh, in_specs=in_specs, out_specs=out_specs, check_vma=False)
```

profile of v0, /device:TPU:10, one launch (start us, length us, event | category | flops | bytes accessed | tf_op | source)
XLA Modules:
  0.0 787.3 jit_solution(18422779835684997760)
XLA Ops:
  9.8 4.9 all-to-all-start
  14.7 5.0 copy.64
  20.3 23.4 %reduce = bf16[4096,128]{1,0:T(8,128)(2,1)} reduce(bf16[4096,1,128]{2,1,0:T(2,128)(2,1)S(1)} %bitcast.85, bf16[]{:T(256)} %broadcast.111), dimensions={1}, to_apply=%bitcast.74.reduce_sub_computation | reduce | bytes 2097154
  47.2 4.8 all-to-all-start.1
  54.0 11.1 %all-to-all-done.1 = bf16[4,2,65536]{2,1,0:T(2,128)(2,1)} async-done(((bf16[4,2,65536]{2,1,0:T(2,128)(2,1)}), bf16[4,2,65536]{2,1,0:T(2,128)(2,1)}, u32[]{:S(2)}, u32[]{:S(2)}) %all-to-all-start.1) | async-done | bytes 1048608 | tf_op jit(solution)/shard_map/all_to_all | solution.py:118
  71.9 5.5 fusion.33
  81.6 10.2 %fusion.34 = f32[512,4096]{1,0:T(8,128)} fusion(bf16[512,1024]{0,1:T(8,128)(2,1)S(1)} %bitcast.89, bf16[1024,4096]{1,0:T(8,128)(2,1)} %all-gather.2.cloned.1.call-done), kind=kOutput, calls=%fused_computation.59 | convolution fusion | flops 4294967296 | bytes 17825792 | tf_op jit(solution)/shard_map/dot_general | solution.py:124
  93.8 78.8 %reduce-scatter.2.cloned.1.call-done = f32[128,4096]{1,0:T(8,128)} async-done(((f32[512,4096]{1,0:T(8,128)}), f32[128,4096]{1,0:T(8,128)}) %reduce-scatter.2.cloned.1.call-update) | async-done | bytes 2097168 | tf_op jit(solution)/shard_map/reduce_scatter | solution.py:123
  176.5 17.4 %scatter_custom_fusion = bf16[1280,4096]{1,0:T(8,128)(2,1)} fusion(s32[1024]{0:T(1024)S(1)} %bitcast.95, bf16[]{:T(256)} %constant.25.clone.1, bf16[128,4096]{1,0:T(8,128)(2,1)S(1)} %multiply_convert_fusion), kind=kCustom, calls=%fused_computation.12 | custom fusion | bytes 11534338 | tf_op jit(solution)/shard_map/scatter | solution.py:138
  193.9 15.4 %reshape.139 = bf16[128,10,4096]{2,1,0:T(8,128)(2,1)} reshape(bf16[1280,4096]{1,0:T(8,128)(2,1)} %scatter_custom_fusion) | data formatting | bytes 20971520 | tf_op jit(solution)/shard_map/reshape | solution.py:140
  209.2 199.3 %all_to_all.45 = bf16[128,10,4096]{2,1,0:T(8,128)(2,1)} all-to-all(bf16[128,10,4096]{2,1,0:T(8,128)(2,1)} %reshape.139), channel_id=1, replica_groups=mesh['seq'=4,'exp'=32] {'seq','exp'}, dimensions={0} | all-to-all | bytes 20971520 | tf_op jit(solution)/shard_map/all_to_all | solution.py:139
  408.5 16.6 %reshape.140 = bf16[1280,4096]{1,0:T(8,128)(2,1)} reshape(bf16[128,10,4096]{2,1,0:T(8,128)(2,1)} %all_to_all.45) | data formatting | bytes 20971520 | tf_op jit(solution)/shard_map/reshape | solution.py:146
  425.1 20.1 %fusion.1 = f32[1280,1536]{1,0:T(8,128)S(1)} fusion(bf16[1280,4096]{1,0:T(8,128)(2,1)} %reshape.140, bf16[1,4096,1536]{2,1,0:T(8,128)(2,1)} %param.22), kind=kOutput, calls=%fused_computation.6 | convolution fusion | flops 16106127360 | bytes 30932992 | tf_op jit(solution)/shard_map/dot_general | solution.py:149
  445.2 10.7 %convolution_convert_fusion = bf16[1280,4096]{1,0:T(8,128)(2,1)} fusion(bf16[1,768,4096]{2,1,0:T(8,128)(2,1)S(1)} %bitcast.101, f32[1280,1536]{1,0:T(8,128)S(1)} %fusion.1), kind=kOutput, calls=%fused_computation.5 | convolution fusion | flops 8064204800 | bytes 24641536 | tf_op jit(solution)/shard_map/dot_general | solution.py:151
  455.9 15.1 %reshape_reshape.6 = bf16[128,1,10,4096]{3,2,0,1:T(8,128)(2,1)} reshape(bf16[1280,4096]{1,0:T(8,128)(2,1)} %convolution_convert_fusion) | data formatting | bytes 20971520 | tf_op jit(solution)/shard_map/reshape;reshape | solution.py:30
  471.0 12.3 %slice_bitcast_fusion.1 = (bf16[128,1,5,4096]{3,2,1,0:T(8,128)(2,1)S(1)}, bf16[128,1,5,4096]{3,2,1,0:T(8,128)(2,1)}) fusion(bf16[128,1,10,4096]{3,2,0,1:T(8,128)(2,1)} %reshape_reshape.6), kind=kLoop, calls=%fused_computation.9 | loop fusion | bytes 20971520 | tf_op jit(solution)/shard_map/split | solution.py:49
  483.4 107.4 %all_to_all.46 = bf16[128,1,5,4096]{3,2,1,0:T(8,128)(2,1)} all-to-all(bf16[128,1,5,4096]{3,2,1,0:T(8,128)(2,1)S(1)} %get-tuple-element.16), channel_id=1, replica_groups=mesh['seq'=4,'exp'=32] {'seq','exp'}, dimensions={0} | all-to-all | bytes 10485760 | tf_op jit(solution)/shard_map/all_to_all | solution.py:51
  590.8 6.3 all-to-all-start.4
  597.3 104.4 %all-to-all-done.4 = bf16[128,1,5,4096]{3,2,1,0:T(8,128)(2,1)} async-done(((bf16[128,1,5,4096]{3,2,1,0:T(8,128)(2,1)}), bf16[128,1,5,4096]{3,2,1,0:T(8,128)(2,1)}, u32[]{:S(2)}, u32[]{:S(2)}) %all-to-all-start.4) | async-done | bytes 5242912 | tf_op jit(solution)/shard_map/all_to_all | solution.py:51
  701.6 15.7 %pad_maximum_fusion = bf16[128,1,10,4096]{3,2,1,0:T(8,128)(2,1)} fusion(bf16[128,1,5,4096]{3,2,1,0:T(8,128)(2,1)} %all-to-all-done.4, bf16[128,1,5,4096]{3,2,1,0:T(8,128)(2,1)} %all_to_all.46), kind=kLoop, calls=%fused_computation.3 | loop fusion | flops 20971520 | bytes 20971520 | tf_op jit(solution)/shard_map/concatenate | solution.py:52
  717.3 16.5 %reshape_reshape.7 = bf16[1280,4096]{1,0:T(8,128)(2,1)} reshape(bf16[128,1,10,4096]{3,2,1,0:T(8,128)(2,1)} %pad_maximum_fusion) | data formatting | bytes 20971520 | tf_op jit(solution)/shard_map/reshape;reshape | solution.py:157
  733.8 20.5 %gather_fusion = bf16[1024,4096]{1,0:T(8,128)(2,1)} fusion(bf16[1280,4096]{1,0:T(8,128)(2,1)} %reshape_reshape.7, s32[1024]{0:T(1024)S(1)} %broadcast_clamp_fusion), kind=kCustom, calls=%fused_computation | custom fusion | bytes 16781312 | tf_op jit(solution)/shard_map/gather | solution.py:158
  754.3 13.1 %multiply_reduce_fusion = f32[128,4096]{1,0:T(8,128)} fusion(bf16[1024,4096]{1,0:T(8,128)(2,1)} %gather_fusion, f32[128,8]{1,0:T(8,128)S(1)} %copy.68), kind=kLoop, calls=%fused_computation.4 | loop fusion | flops 12058624 | bytes 10489856 | tf_op jit(solution)/shard_map/reduce_sum | solution.py:160
  767.5 9.0 %fusion.3 = f32[128,1,8]{2,1,0:T(1,128)S(1)} fusion(bf16[1024,4096]{1,0:T(8,128)(2,1)} %gather_fusion, bf16[128,4096,1]{1,0,2:T(8,128)(2,1)S(1)} %bitcast.83), kind=kOutput, calls=%fused_computation.10 | convolution fusion | flops 8388608 | bytes 9441280 | tf_op jit(solution)/shard_map/tkd,td->tk/dot_general | solution.py:162
  (64 shorter events, 29.4 us)
Async XLA Ops:
  7.2 760.3 %copy-start = (bf16[1,128,4096]{2,1,0:T(8,128)(2,1)S(1)}, bf16[1,128,4096]{2,1,0:T(8,128)(2,1)}, u32[]{:S(2)}) copy-start(bf16[1,128,4096]{2,1,0:T(8,128)(2,1)} %param.21) | copy-start | bytes 3145732
  7.2 45.0 %copy-start.7 = (s32[1,512]{1,0:T(1,128)S(1)}, s32[1,512]{1,0:T(1,128)}, u32[]{:S(2)}) copy-start(s32[1,512]{1,0:T(1,128)} %param.15) | copy-start | bytes 6148
  7.2 74.4 %all-gather.2.cloned.1.call-start = ((), (), s32[]{:S(2)}) async-start(), calls=%async_computation.6 | async-start | bytes 8650752 | tf_op jit(solution)/shard_map/all_gather | solution.py:122
  9.8 37.4 %all-to-all-start = ((bf16[2,128,512]{1,0,2:T(2,128)(2,1)}), bf16[2,128,512]{1,0,2:T(2,128)(2,1)S(1)}, u32[]{:S(2)}, u32[]{:S(2)}) async-start(bf16[2,128,512]{1,0,2:T(2,128)(2,1)} %copy.61), calls=%async_computation | async-start | bytes 524288 | tf_op jit(solution)/shard_map/all_to_all | solution.py:21
  47.2 17.9 %all-to-all-start.1 = ((bf16[4,2,65536]{2,1,0:T(2,128)(2,1)}), bf16[4,2,65536]{2,1,0:T(2,128)(2,1)}, u32[]{:S(2)}, u32[]{:S(2)}) async-start(bf16[4,2,65536]{2,1,0:T(2,128)(2,1)} %reshape.165), calls=%async_computation.1 | async-start | bytes 2097152 | tf_op jit(solution)/shard_map/all_to_all | solution.py:118
  52.0 120.6 %reduce-scatter.2.cloned.1.call-start = ((), (), s32[]{:S(2)}) async-start(), calls=%async_computation.7 | async-start | bytes 10485760 | tf_op jit(solution)/shard_map/reduce_scatter | solution.py:123
  67.7 4.2 copy-start.3
  71.9 5.5 copy-start.4
  91.7 0.7 copy-start.6
  91.7 80.9 %copy-start.2 = (bf16[1,128,4096]{2,1,0:T(8,128)(2,1)S(1)}, bf16[1,128,4096]{2,1,0:T(8,128)(2,1)}, u32[]{:S(2)}) copy-start(bf16[1,128,4096]{2,1,0:T(8,128)(2,1)} %param.16) | copy-start | bytes 3145732
  91.7 82.8 %copy-start.5 = (f32[4096]{0:T(1024)S(1)}, f32[4096]{0:T(1024)}, u32[]{:S(2)}) copy-start(f32[4096]{0:T(1024)} %param.18) | copy-start | bytes 49156
  408.5 36.7 %slice-start = ((s8[6291456]{0:T(1024)(128)(4,1)}), s8[2097152]{0:T(1024)(128)(4,1)S(1)}, s32[]{:S(2)}) async-start(s8[6291456]{0:T(1024)(128)(4,1)} %bitcast.100), calls=%async_computation.8 | async-start | bytes 4194304
  425.1 20.1 %slice-start.1 = ((s8[6291456]{0:T(1024)(128)(4,1)}), s8[4194304]{0:T(1024)(128)(4,1)S(1)}, s32[]{:S(2)}) async-start(s8[6291456]{0:T(1024)(128)(4,1)} %bitcast.100), calls=%async_computation.9 | async-start | bytes 8388608
  590.8 6.3 copy-start.8
  590.8 110.8 %all-to-all-start.4 = ((bf16[128,1,5,4096]{3,2,1,0:T(8,128)(2,1)}), bf16[128,1,5,4096]{3,2,1,0:T(8,128)(2,1)}, u32[]{:S(2)}, u32[]{:S(2)}) async-start(bf16[128,1,5,4096]{3,2,1,0:T(8,128)(2,1)} %get-tuple-element.17), calls=%async_computation.5 | async-start | bytes 16777216 | tf_op jit(solution)/shard_map/all_to_all | solution.py:51
  767.5 9.7 %copy-start.1 = (f32[128,4096]{1,0:T(8,128)S(1)}, f32[128,4096]{1,0:T(8,128)}, u32[]{:S(2)}) copy-start(f32[128,4096]{1,0:T(8,128)} %reduce-scatter.2.cloned.1.call-done) | copy-start | bytes 6291460
Sparse Core Ops, SparseCore 0:
  10.2 60.8 all-gather.1
  91.9 80.6 reduce-scatter.1
where the time goes:
time: 794 us; the launch traced here: 787 us
  blocking collectives  307 us (39%)
  waiting for transfers between devices  195 us (25%)
  local copies, waits for them, and re-layouts  132 us (17%)
  other arithmetic  67.2 us (8%)
  matrix products  55.3 us (7%)
  starting transfers between devices  16.2 us (2%)
  between operations  14.5 us (2%)
    all_to_all x1, blocking collectives, shards(): lax.all_to_all(outgoing.reshape(experts, capacity, model_width), ('seq',...  199 us
    all_to_all x1, blocking collectives, several_exchanges(): lax.all_to_all(piece, axis, split_axis=0, concat_axis=0, tiled=True)  107 us
    all_to_all x1, waiting for transfers between devices, several_exchanges(): lax.all_to_all(piece, axis, split_axis=0, concat_axis=0, tiled=True)  104 us
    reduce_scatter x1, waiting for transfers between devices, shards(): lax.psum_scatter(jnp.dot(attended, full_rows, preferred_element_type=jnp....  78.8 us
    unnamed x2, other arithmetic  23.4 us
    gather x1, local copies, waits for them, and re-layouts, shards(): picked = returned[target].reshape(token_count, top_count, model_width)  20.5 us
    dot_general x1, matrix products, shards(): gate_up = jnp.dot(incoming, weight_in, preferred_element_type=jnp.float32)  20.1 us
    scatter x1, local copies, waits for them, and re-layouts, shards(): jnp.zeros((slot_limit, model_width), jnp.bfloat16).at[target].set(sources)  17.4 us
  transfers between devices with their start and end apart: 5, of which 3 were waited for; matrix products, arithmetic and copies ran while one was open for 7% of the time, Pallas kernels for 0%

commit v1 on v0

v1 whole, which is shorter than its diff:
```python
import math

import jax
import jax.numpy as jnp
from jax import lax
from jax.experimental import pallas as pl
from jax.experimental.pallas import tpu as pltpu
from jax.sharding import PartitionSpec as P

QUERY_HEADS = 32
KEY_VALUE_HEADS = 4
HEAD_SIZE = 128
MAIN = 8
EXTRA = 2
QUARTERS = 4
BF = jnp.bfloat16
F32 = jnp.float32
VMEM_LIMIT = 60 * 1024 * 1024


def dot(a, b):
    return jnp.dot(a, b, preferred_element_type=F32)


def attend_heads(q_heads, k_heads, v_heads, doc_rows):
    length = q_heads.shape[0]
    group = QUERY_HEADS // KEY_VALUE_HEADS
    score_scale = 1.0 / math.sqrt(HEAD_SIZE)
    positions = jnp.arange(length)
    allowed = (positions[None, :] <= positions[:, None]) & (doc_rows[None, :] == doc_rows[:, None])
    query_block = q_heads.reshape(length, group, HEAD_SIZE)
    scores = jnp.einsum("rgd,jd->grj", query_block, k_heads, preferred_element_type=F32) * score_scale
    scores = jnp.where(allowed[None], scores, -jnp.inf)
    row_max = jnp.max(scores, axis=-1, keepdims=True)
    raised = jnp.exp(scores - row_max)
    weights_bf = (raised / jnp.sum(raised, axis=-1, keepdims=True)).astype(BF)
    block_out = jnp.einsum("grj,jd->rgd", weights_bf, v_heads, preferred_element_type=F32)
    return block_out.astype(BF).reshape(length, group * HEAD_SIZE)


def pack_kernel(projected, residual, gain, main_hot, extra_hot, hidden, out, stacked):
    step = pl.program_id(0)
    tokens = residual.shape[0]
    quarter = stacked.shape[1]

    @pl.when(step == 0)
    def _():
        state = residual[...].astype(F32) + projected[...].astype(F32)
        hidden[...] = state
        mean = jnp.mean(state * state, axis=-1, keepdims=True)
        normed = (state / jnp.sqrt(mean + 1e-06) * gain[...]).astype(BF)
        for c in range(QUARTERS):
            stacked[c * tokens : (c + 1) * tokens, :] = normed[:, c * quarter : (c + 1) * quarter]

    @pl.when(step < QUARTERS)
    def _():
        rows = stacked[pl.ds(pl.multiple_of(step * tokens, tokens), tokens), :]
        out[...] = dot(main_hot[...], rows).astype(BF)

    @pl.when(step == QUARTERS)
    def _():
        out[...] = dot(extra_hot[...], stacked[...]).astype(BF)


def pack(projected, residual, gain, main_hot, extra_hot):
    tokens, width = residual.shape
    quarter = width // QUARTERS
    slots = main_hot.shape[0]
    whole = lambda shape: pl.BlockSpec(shape, lambda i: (0, 0))
    return pl.pallas_call(
        pack_kernel,
        grid=(QUARTERS + 1,),
        in_specs=[
            whole((tokens, width)),
            whole((tokens, width)),
            whole((1, width)),
            whole(main_hot.shape),
            whole(extra_hot.shape),
        ],
        out_specs=[whole((tokens, width)), pl.BlockSpec((slots, quarter), lambda i: (0, i))],
        out_shape=[
            jax.ShapeDtypeStruct((tokens, width), F32),
            jax.ShapeDtypeStruct((slots, width + quarter), BF),
        ],
        scratch_shapes=[pltpu.VMEM((QUARTERS * tokens, quarter), BF)],
        compiler_params=pltpu.CompilerParams(vmem_limit_bytes=VMEM_LIMIT),
        name="norm_pack",
    )(projected, residual, gain, main_hot, extra_hot)


def regroup_matrix(transposed):
    size = 32 * QUARTERS * EXTRA
    grouped = lax.broadcasted_iota(jnp.int32, (size, size), 1 if transposed else 0)
    plain = lax.broadcasted_iota(jnp.int32, (size, size), 0 if transposed else 1)
    c, rest = grouped // (32 * EXTRA), grouped % (32 * EXTRA)
    source = (rest // EXTRA) * (QUARTERS * EXTRA) + c * EXTRA + rest % EXTRA
    return (source == plain).astype(F32).astype(BF)


def expert_kernel(main, extra, w_in, w_down, out, acc, act, parts):
    step = pl.program_id(0)
    slots = main.shape[0]
    hidden = act.shape[1]
    extras = parts.shape[1]
    groups = slots // 256
    per = extras // groups

    @pl.when(step == 0)
    def _():
        swap = regroup_matrix(False)
        for g in range(groups):
            rows = dot(swap, extra[g * 256 : (g + 1) * 256, :]).astype(BF)
            for c in range(QUARTERS):
                parts[c, g * per : (g + 1) * per, :] = rows[c * per : (c + 1) * per, :]

    @pl.when(step == 0)
    def _():
        acc[:slots, :] = dot(main[...], w_in[...])
        acc[slots:, :] = dot(parts[0], w_in[...])

    @pl.when((step > 0) & (step < QUARTERS))
    def _():
        acc[:slots, :] += dot(main[...], w_in[...])
        acc[slots:, :] += dot(parts[step], w_in[...])

    @pl.when(step == QUARTERS - 1)
    def _():
        gate = acc[:, :hidden]
        act[...] = (gate / (1.0 + jnp.exp(-gate)) * acc[:, hidden:]).astype(BF)

    @pl.when((step >= QUARTERS) & (step < 2 * QUARTERS))
    def _():
        out[...] = dot(act[:slots, :], w_down[...]).astype(BF)
        parts[step - QUARTERS] = dot(act[slots:, :], w_down[...]).astype(BF)

    @pl.when(step == 2 * QUARTERS)
    def _():
        swap = regroup_matrix(True)
        for g in range(groups):
            rows = jnp.concatenate([parts[c, g * per : (g + 1) * per, :] for c in range(QUARTERS)], axis=0)
            out[g * 256 : (g + 1) * 256, :] = dot(swap, rows).astype(BF)


def run_expert(incoming, w_in, w_down):
    slots = incoming.shape[0]
    width = w_in.shape[0]
    hidden = w_down.shape[0]
    quarter = width // QUARTERS
    extras = slots // MAIN * EXTRA
    last = QUARTERS - 1
    return pl.pallas_call(
        expert_kernel,
        grid=(2 * QUARTERS + 1,),
        in_specs=[
            pl.BlockSpec((slots, quarter), lambda i: (0, jnp.minimum(i, last))),
            pl.BlockSpec((slots, quarter), lambda i: (0, QUARTERS)),
            pl.BlockSpec((quarter, 2 * hidden), lambda i: (jnp.minimum(i, last), 0)),
            pl.BlockSpec((hidden, quarter), lambda i: (0, jnp.clip(i - QUARTERS, 0, last))),
        ],
        out_specs=pl.BlockSpec((slots, quarter), lambda i: (0, jnp.maximum(i - QUARTERS, 0))),
        out_shape=jax.ShapeDtypeStruct((slots, width + quarter), BF),
        scratch_shapes=[
            pltpu.VMEM((slots + extras, 2 * hidden), F32),
            pltpu.VMEM((slots + extras, hidden), BF),
            pltpu.VMEM((QUARTERS, extras, quarter), BF),
        ],
        compiler_params=pltpu.CompilerParams(vmem_limit_bytes=VMEM_LIMIT),
        name="experts",
    )(incoming, incoming, w_in, w_down)


def combine_kernel(main, extra, hidden, cot, gates_main, gates_extra, keys_main, keys_extra, out, grad, dots_main, dots_extra):
    step = pl.program_id(0)
    tokens = hidden.shape[0]
    slots = main.shape[0]
    of_quarter = lax.broadcasted_iota(jnp.int32, (1, slots), 1) % (QUARTERS * EXTRA) // EXTRA == step
    from_main = dot(gates_main[...], main[...])
    weights = jnp.where(of_quarter, gates_extra[...].astype(F32), 0.0).astype(BF)
    from_extra = dot(weights, extra[...])
    mixed = hidden[...] + (from_main[:tokens] + from_main[tokens:] + from_extra[:tokens] + from_extra[tokens:])
    out[...] = mixed.astype(BF)
    contract_last = (((1,), (1,)), ((), ()))
    new_main = lax.dot_general(cot[...], main[...], contract_last, preferred_element_type=F32)
    new_extra = lax.dot_general(cot[...], extra[...], contract_last, preferred_element_type=F32)
    new_extra = jnp.where(of_quarter, new_extra, 0.0)

    @pl.when(step == 0)
    def _():
        dots_main[...] = new_main
        dots_extra[...] = new_extra

    @pl.when(step > 0)
    def _():
        dots_main[...] += new_main
        dots_extra[...] += new_extra

    @pl.when(step == QUARTERS - 1)
    def _():
        slot = lax.broadcasted_iota(jnp.int32, (tokens, slots), 1)
        extra_slot = slot // (QUARTERS * EXTRA) * EXTRA + slot % EXTRA
        sums = []
        for k in range(keys_main.shape[1]):
            picked = jnp.where(slot == keys_main[:, k : k + 1], dots_main[...], 0.0)
            picked += jnp.where(extra_slot == keys_extra[:, k : k + 1], dots_extra[...], 0.0)
            sums.append(jnp.sum(picked, axis=1, keepdims=True))
        grad[...] = jnp.concatenate(sums, axis=1)


def combine(returned, hidden, cot, gates_main, gates_extra, keys_main, keys_extra):
    slots = returned.shape[0]
    tokens, width = hidden.shape
    quarter = width // QUARTERS
    top = keys_main.shape[1]
    whole = lambda shape: pl.BlockSpec(shape, lambda i: (0, 0))
    part = lambda shape: pl.BlockSpec(shape, lambda i: (0, i))
    return pl.pallas_call(
        combine_kernel,
        grid=(QUARTERS,),
        in_specs=[
            part((slots, quarter)),
            pl.BlockSpec((slots, quarter), lambda i: (0, QUARTERS)),
            part((tokens, quarter)),
            part((tokens, quarter)),
            whole(gates_main.shape),
            whole(gates_extra.shape),
            whole(keys_main.shape),
            whole(keys_extra.shape),
        ],
        out_specs=[part((tokens, quarter)), whole((tokens, top))],
        out_shape=[jax.ShapeDtypeStruct((tokens, width), BF), jax.ShapeDtypeStruct((tokens, top), F32)],
        scratch_shapes=[pltpu.VMEM((tokens, slots), F32), pltpu.VMEM((tokens, slots), F32)],
        compiler_params=pltpu.CompilerParams(vmem_limit_bytes=VMEM_LIMIT),
        name="combine",
    )(returned, returned, hidden, cot, gates_main, gates_extra, keys_main, keys_extra)


def split_in_two(values):
    high = values.astype(BF)
    return jnp.concatenate([high, (values - high.astype(F32)).astype(BF)], axis=0)


def routing(chosen, gates, experts):
    tokens = chosen.shape[0]
    hits = chosen[:, :, None] == jnp.arange(experts, dtype=jnp.int32)[None, None, :]
    member = jnp.any(hits, axis=1)
    earlier = jnp.arange(tokens)[None, :] < jnp.arange(tokens)[:, None]
    rank = dot(earlier.astype(BF), member.astype(BF)).astype(jnp.int32)
    rank = jnp.where(member, rank, -1)
    gate_of = jnp.sum(jnp.where(hits, gates[:, :, None], 0.0), axis=1)
    pair_rank = jnp.sum(jnp.where(hits, rank[:, None, :], 0), axis=2)

    is_main = rank[:, :, None] == jnp.arange(MAIN, dtype=jnp.int32)
    extra_row = jnp.arange(QUARTERS * EXTRA, dtype=jnp.int32)
    is_extra = rank[:, :, None] == MAIN + extra_row % EXTRA
    main_hot = is_main.astype(BF).transpose(1, 2, 0).reshape(experts * MAIN, tokens)
    in_quarter = extra_row[None, :, None, None] // EXTRA == jnp.arange(QUARTERS)[None, None, :, None]
    extra_hot = (is_extra.transpose(1, 2, 0)[:, :, None, :] & in_quarter).astype(BF)
    extra_hot = extra_hot.reshape(experts * QUARTERS * EXTRA, QUARTERS * tokens)

    gates_main = jnp.where(is_main, gate_of[:, :, None], 0.0).reshape(tokens, experts * MAIN)
    gates_extra = jnp.where(is_extra, gate_of[:, :, None], 0.0).reshape(tokens, experts * QUARTERS * EXTRA)
    keys_main = jnp.where(pair_rank < MAIN, chosen * MAIN + pair_rank, -1)
    keys_extra = jnp.where(pair_rank >= MAIN, chosen * EXTRA + pair_rank - MAIN, -1)
    return main_hot, extra_hot, split_in_two(gates_main), split_in_two(gates_extra), keys_main, keys_extra


def shards(
    queries,
    rotated_keys,
    projected_values,
    doc_ids,
    residual,
    out_weight,
    norm_gain,
    routes,
    gate_vals,
    cotangent,
    expert_in,
    expert_down,
):
    seq_count = lax.axis_size("seq")
    experts = seq_count * lax.axis_size("exp")
    tokens, width = residual.shape[1:]
    full_rows = lax.all_gather(out_weight, "exp", axis=1, tiled=True)

    by_head = lambda a: a[0].reshape(tokens, seq_count, -1)
    heads = jnp.concatenate([by_head(queries), by_head(rotated_keys), by_head(projected_values)], axis=2)
    heads = lax.all_to_all(heads.transpose(1, 0, 2), "seq", split_axis=0, concat_axis=0, tiled=True)
    heads = heads.reshape(seq_count * tokens, -1)
    q_width = width // seq_count
    attended = attend_heads(
        heads[:, :q_width],
        heads[:, q_width : q_width + HEAD_SIZE],
        heads[:, q_width + HEAD_SIZE :],
        doc_ids[0],
    )
    partial = dot(attended, full_rows).astype(BF)
    projected = lax.psum_scatter(partial, "seq", scatter_dimension=0, tiled=True)

    main_hot, extra_hot, gates_main, gates_extra, keys_main, keys_extra = routing(routes[0], gate_vals[0], experts)
    hidden, outgoing = pack(projected, residual[0], norm_gain[None, :], main_hot, extra_hot)

    def exchange(slots):
        blocks = slots.reshape(experts, MAIN, slots.shape[1])
        blocks = lax.all_to_all(blocks, ("seq", "exp"), split_axis=0, concat_axis=0, tiled=True)
        return blocks.reshape(slots.shape)

    results = run_expert(exchange(outgoing), expert_in[0], expert_down[0])
    layer_out, gate_grad = combine(
        exchange(results), hidden, cotangent[0], gates_main, gates_extra, keys_main, keys_extra
    )
    return layer_out[None], gate_grad[None]


def solution(mesh):
    in_specs = (
        P("exp", "seq", None),
        P("exp", "seq", None),
        P("exp", "seq", None),
        P("exp", None),
        P("exp", "seq", None),
        P("seq", "exp"),
        P(),
        P("exp", "seq", None),
        P("exp", "seq", None),
        P("exp", "seq", None),
        P(("seq", "exp"), None, None),
        P(("seq", "exp"), None, None),
    )
    out_specs = (P("exp", "seq", None), P("exp", "seq", None))
    return jax.shard_map(shards, mesh=mesh, in_specs=in_specs, out_specs=out_specs, check_vma=False)
```

time: 794 us -> 468 us (0.59)
  blocking collectives: 307 us -> 128 us
  local copies, waits for them, and re-layouts: 132 us -> 7.39 us
  Pallas kernels: 0 us -> 60.8 us
  other arithmetic: 67.2 us -> 9.43 us
  matrix products: 55.3 us -> 19.6 us
  waiting for transfers between devices: 195 us -> 210 us
    all_to_all x2 -> x1, blocking collectives: 307 us -> 128 us  [exchange(): lax.all_to_all(blocks, ('seq', 'exp'), split_axis=0, concat_axis=0, tiled...]
    pallas_call x0 -> x3, Pallas kernels: none -> 60.8 us  [the longest x1 34.5 us: run_expert(): pl.pallas_call(expert_kernel, grid=(2 * QUARTERS + 1,), in_specs=[pl.Bloc...]
    dot_general x6 -> x3, matrix products: 55.3 us -> 13.8 us  [the longest x2 9.63 us: dot(): return jnp.dot(a, b, preferred_element_type=F32)]
    reduce_scatter x1, waiting for transfers between devices: 78.8 us -> 42.6 us  [shards(): lax.psum_scatter(partial, 'seq', scatter_dimension=0, tiled=True)]
    reshape x2 -> x0, local copies, waits for them, and re-layouts: 32 us -> none  [the longest x1 16.6 us: shards(): incoming = incoming.reshape(slot_limit, model_width)]
    another operation x5 -> x6, local copies, waits for them, and re-layouts: 31.7 us -> 4.08 us  [shards(): by_head = lambda a: a[0].reshape(tokens, seq_count, -1)]
    all_gather x1, waiting for transfers between devices: 0.02 us -> 25.8 us  [shards(): full_rows = lax.all_gather(out_weight, 'exp', axis=1, tiled=True)]
    all_to_all x3 -> x2, waiting for transfers between devices: 116 us -> 141 us  [the longest x1 126 us: exchange(): lax.all_to_all(blocks, ('seq', 'exp'), split_axis=0, concat_axis=0, tiled...]
  transfers between devices with their start and end apart: 5 -> 4, of which waited for: 3 -> 4; matrix products, arithmetic and copies ran while one was open for 7% -> 6% of each run, Pallas kernels for 0% -> 0%
where the time goes in v1:
time: 468 us; the launch traced here: 462 us
  waiting for transfers between devices  210 us (45%)
  blocking collectives  128 us (27%)
  Pallas kernels  60.8 us (13%)
  matrix products  19.6 us (4%)
  between operations  14.3 us (3%)
  starting transfers between devices  12.3 us (3%)
  other arithmetic  9.43 us (2%)
  local copies, waits for them, and re-layouts  7.39 us (2%)
    all_to_all x1, blocking collectives, exchange(): lax.all_to_all(blocks, ('seq', 'exp'), split_axis=0, concat_axis=0, tiled...  128 us
    all_to_all x1, waiting for transfers between devices, exchange(): lax.all_to_all(blocks, ('seq', 'exp'), split_axis=0, concat_axis=0, tiled...  126 us
    reduce_scatter x1, waiting for transfers between devices, shards(): lax.psum_scatter(partial, 'seq', scatter_dimension=0, tiled=True)  42.6 us
    pallas_call x1, Pallas kernels, run_expert(): pl.pallas_call(expert_kernel, grid=(2 * QUARTERS + 1,), in_specs=[pl.Bloc...  34.5 us
    all_gather x1, waiting for transfers between devices, shards(): full_rows = lax.all_gather(out_weight, 'exp', axis=1, tiled=True)  25.8 us
    pallas_call x1, Pallas kernels, combine(): pl.pallas_call(combine_kernel, grid=(QUARTERS,), in_specs=[part((slots, q...  16 us
    all_to_all x1, waiting for transfers between devices, shards(): lax.all_to_all(heads.transpose(1, 0, 2), 'seq', split_axis=0, concat_axis...  15.5 us
    pallas_call x1, Pallas kernels, pack(): pl.pallas_call(pack_kernel, grid=(QUARTERS + 1,), in_specs=[whole((tokens...  10.3 us
  transfers between devices with their start and end apart: 4, of which 4 were waited for; matrix products, arithmetic and copies ran while one was open for 6% of the time, Pallas kernels for 0%

profile of v1, /device:TPU:10, one launch (start us, length us, event | category | flops | bytes accessed | tf_op | source)
XLA Modules:
  0.0 462.4 jit_solution(5557618547332461244)
XLA Ops:
  7.9 0.9 reshape_squeeze.11
  8.9 0.9 reshape_squeeze.10
  9.8 1.9 reshape_squeeze.9
  12.0 1.2 maximum_bitcast_fusion
  13.3 4.9 %all-to-all-start = ((bf16[4,128,1280]{2,1,0:T(8,128)(2,1)}), bf16[4,128,1280]{2,1,0:T(8,128)(2,1)S(1)}, u32[]{:S(2)}, u32[]{:S(2)}) async-start(bf16[4,128,1280]{2,1,0:T(8,128)(2,1)} %maximum_bitcast_fusion), calls=%async_computation | async-start | bytes 2621440 | tf_op jit(solution)/shard_map/all_to_all | solution.py:288
  18.2 0.9 fusion.9
  19.1 15.5 %all-to-all-done = bf16[4,128,1280]{2,1,0:T(8,128)(2,1)S(1)} async-done(((bf16[4,128,1280]{2,1,0:T(8,128)(2,1)}), bf16[4,128,1280]{2,1,0:T(8,128)(2,1)S(1)}, u32[]{:S(2)}, u32[]{:S(2)}) %all-to-all-start) | async-done | bytes 1310752 | tf_op jit(solution)/shard_map/all_to_all | solution.py:288
  35.3 5.8 %fusion.20 = (f32[8,512]{1,0:T(8,128)S(1)}, f32[8,512,512]{1,2,0:T(8,128)}) fusion(pred[512,512]{0,1:T(8,128)(4,1)} %fusion.9, bf16[512,8,128]{0,2,1:T(8,128)(2,1)S(1)} %bitcast.80, bf16[512,1280]{1,0:T(8,128)(2,1)S(1)} %bitcast.72), kind=kOutput, calls=%fused_computation.51 | convolution fusion | flops 545260032 | bytes 9846784 | tf_op jit(solution)/shard_map/sub | solution.py:35
  41.1 4.2 fusion.6
  45.3 25.8 %all-gather.2.cloned.1.call-done = bf16[1024,4096]{1,0:T(8,128)(2,1)} async-done(((bf16[1024,128]{1,0:T(8,128)(2,1)}), bf16[1024,4096]{1,0:T(8,128)(2,1)}) %all-gather.2.cloned.1.call-update) | async-done | bytes 8388624 | tf_op jit(solution)/shard_map/all_gather | solution.py:284
  71.1 9.5 %convolution_convert_fusion = bf16[512,4096]{1,0:T(8,128)(2,1)} fusion(bf16[512,1024]{0,1:T(8,128)(2,1)S(1)} %bitcast.86, bf16[1024,4096]{1,0:T(8,128)(2,1)} %all-gather.2.cloned.1.call-done), kind=kOutput, calls=%fused_computation.5 | convolution fusion | flops 4297064448 | bytes 13631488 | tf_op jit(solution)/shard_map/dot_general | solution.py:22
  81.5 0.9 fusion.13.main_hot
  82.4 1.2 fusion.8.extra_hot
  83.7 42.6 %reduce-scatter.2.cloned.1.call-done.projected = bf16[128,4096]{1,0:T(8,128)(2,1)} async-done(((bf16[512,4096]{1,0:T(8,128)(2,1)}), bf16[128,4096]{1,0:T(8,128)(2,1)}) %reduce-scatter.2.cloned.1.call-update) | async-done | bytes 1048592 | tf_op jit(solution)/shard_map/reduce_scatter | solution.py:298
  126.3 10.3 %norm_pack.1 = (f32[128,4096]{1,0:T(8,128)}, bf16[1024,5120]{1,0:T(8,128)(2,1)}) custom-call(bf16[128,4096]{1,0:T(8,128)(2,1)} %reduce-scatter.2.cloned.1.call-done.projected, bf16[128,4096]{1,0:T(8,128)(2,1)} %bitcast.79, f32[1,4096]{1,0:T(1,128)} %bitcast.82, bf16[1024,128]{1,0:T(8,128)(2,1)} %fusion.13.main_hot, bf16[1024,512]{1,0:T(8,128)(2,1)} %fusion.8.extra_hot), custom_call_target="tpu_custom_call" | custom-call | tf_op jit(solution)/shard_map/norm_pack/pallas_call | solution.py:70
  136.5 128.5 %all_to_all.15 = bf16[128,8,5120]{2,1,0:T(8,128)(2,1)} all-to-all(bf16[128,8,5120]{2,1,0:T(8,128)(2,1)} %bitcast.69), channel_id=1, replica_groups=mesh['seq'=4,'exp'=32] {'seq','exp'}, dimensions={0} | all-to-all | bytes 20971520 | tf_op jit(solution)/shard_map/all_to_all | solution.py:305
  265.0 34.5 %experts.1 = bf16[1024,5120]{1,0:T(8,128)(2,1)} custom-call(bf16[1024,5120]{1,0:T(8,128)(2,1)} %bitcast.65, bf16[1024,5120]{1,0:T(8,128)(2,1)} %bitcast.66, bf16[4096,1536]{1,0:T(8,128)(2,1)} %bitcast.68, bf16[768,4096]{1,0:T(8,128)(2,1)} %bitcast.70), custom_call_target="tpu_custom_call" | custom-call | tf_op jit(solution)/shard_map/experts/pallas_call | solution.py:151
  299.6 7.4 %all-to-all-start.2 = ((bf16[128,8,5120]{2,1,0:T(8,128)(2,1)}), bf16[128,8,5120]{2,1,0:T(8,128)(2,1)}, u32[]{:S(2)}, u32[]{:S(2)}) async-start(bf16[128,8,5120]{2,1,0:T(8,128)(2,1)} %bitcast.67), calls=%async_computation.3 | async-start | bytes 20971520 | tf_op jit(solution)/shard_map/all_to_all | solution.py:305
  308.4 1.1 pad_maximum_fusion
  309.5 2.4 select_reduce_fusion
  311.9 0.7 add_select_fusion
  312.6 125.6 %all-to-all-done.2 = bf16[128,8,5120]{2,1,0:T(8,128)(2,1)} async-done(((bf16[128,8,5120]{2,1,0:T(8,128)(2,1)}), bf16[128,8,5120]{2,1,0:T(8,128)(2,1)}, u32[]{:S(2)}, u32[]{:S(2)}) %all-to-all-start.2) | async-done | bytes 10485792 | tf_op jit(solution)/shard_map/all_to_all | solution.py:305
  438.1 16.0 %combine.1 = (bf16[128,4096]{1,0:T(8,128)(2,1)}, f32[128,8]{1,0:T(8,128)}) custom-call(bf16[1024,5120]{1,0:T(8,128)(2,1)} %bitcast.20.main.extra, bf16[1024,5120]{1,0:T(8,128)(2,1)} %bitcast.20.main.extra, f32[128,4096]{1,0:T(8,128)} %get-tuple-element.7.hidden, bf16[128,4096]{1,0:T(8,128)(2,1)} %bitcast.77, bf16[256,1024]{1,0:T(8,128)(2,1)} %get-tuple-element.24.gates_main, ...), custom_call_target="tpu_custom_call" | custom-call | tf_op jit(solution)/shard_map/combine/pallas_call | solution.py:216
  454.1 1.5 copy.55
  (37 shorter events, 4.1 us)
Async XLA Ops:
  7.2 11.0 %copy-start = (s32[1,512]{1,0:T(1,128)S(1)}, s32[1,512]{1,0:T(1,128)}, u32[]{:S(2)}) copy-start(s32[1,512]{1,0:T(1,128)} %param.15) | copy-start | bytes 6148
  7.2 63.9 %all-gather.2.cloned.1.call-start = ((), (), s32[]{:S(2)}) async-start(), calls=%async_computation.4 | async-start | bytes 8650752 | tf_op jit(solution)/shard_map/all_gather | solution.py:284
  13.3 21.4 %all-to-all-start = ((bf16[4,128,1280]{2,1,0:T(8,128)(2,1)}), bf16[4,128,1280]{2,1,0:T(8,128)(2,1)S(1)}, u32[]{:S(2)}, u32[]{:S(2)}) async-start(bf16[4,128,1280]{2,1,0:T(8,128)(2,1)} %maximum_bitcast_fusion), calls=%async_computation | async-start | bytes 2621440 | tf_op jit(solution)/shard_map/all_to_all | solution.py:288
  18.2 108.1 %reduce-scatter.2.cloned.1.call-start = ((), (), s32[]{:S(2)}) async-start(), calls=%async_computation.5 | async-start | bytes 5242880 | tf_op jit(solution)/shard_map/reduce_scatter | solution.py:298
  71.1 9.6 %copy-start.1 = (s32[1,128,8]{1,2,0:T(8,128)S(1)}, s32[1,128,8]{1,2,0:T(8,128)}, u32[]{:S(2)}) copy-start(s32[1,128,8]{1,2,0:T(8,128)} %param.19) | copy-start | bytes 12292
  299.5 7.5 %copy-start.2 = (f32[1,128,8]{1,2,0:T(8,128)S(1)}, f32[1,128,8]{1,2,0:T(8,128)}, u32[]{:S(2)}) copy-start(f32[1,128,8]{1,2,0:T(8,128)} %param.20) | copy-start | bytes 12292
  299.6 138.6 %all-to-all-start.2 = ((bf16[128,8,5120]{2,1,0:T(8,128)(2,1)}), bf16[128,8,5120]{2,1,0:T(8,128)(2,1)}, u32[]{:S(2)}, u32[]{:S(2)}) async-start(bf16[128,8,5120]{2,1,0:T(8,128)(2,1)} %bitcast.67), calls=%async_computation.3 | async-start | bytes 20971520 | tf_op jit(solution)/shard_map/all_to_all | solution.py:305
Sparse Core Ops, SparseCore 0:
  10.2 60.8 all-gather.1
  80.7 45.5 reduce-scatter.1

commit v2 on v1

--- a/solution.py
+++ b/solution.py
@@ -16,6 +16,8 @@
 BF = jnp.bfloat16
 F32 = jnp.float32
 VMEM_LIMIT = 60 * 1024 * 1024
+RING = 4
+CORES = 2
 
 
 def dot(a, b):
@@ -38,19 +40,120 @@
     return block_out.astype(BF).reshape(length, group * HEAD_SIZE)
 
 
-def pack_kernel(projected, residual, gain, main_hot, extra_hot, hidden, out, stacked):
+def exp_shift(along_z, along_x, other_core=0):
+    def place(z, x, core):
+        return (z % RING * RING + x % RING) * CORES + core % CORES
+
+    return [
+        (place(z, x, core), place(z + along_z, x + along_x, core + other_core))
+        for z in range(RING)
+        for x in range(RING)
+        for core in range(CORES)
+    ]
+
+
+def gather_line(part, shifts):
+    return jnp.stack([part] + [lax.ppermute(part, "exp", shifts(d)) for d in range(1, RING)])
+
+
+def gather_plane(line, shifts):
+    gathered = [line]
+    for d in range(1, RING):
+        gathered.append(lax.ppermute(line, "exp", shifts(d)))
+    return gathered
+
+
+def project_kernel(place, mine, other, *rest):
+    pieces, outs = rest[: 2 * RING], rest[2 * RING : -3]
+    weight, result, arrived = rest[-3:]
+    step = pl.program_id(0)
+    tokens, block = outs[0].shape
+    length = mine.shape[0]
+    half = weight.shape[0] // 2
+
+    @pl.when(step == 0)
+    def _():
+        copies = []
+        for k in range(RING):
+            for m in range(RING):
+                for lower in range(2):
+                    z, x = (m, k) if lower else (k, m)
+                    chip = lax.rem(place[1] + RING - z, RING) * RING + lax.rem(place[2] + RING - x, RING)
+                    lanes = pl.ds(pl.multiple_of(chip * 128, 128), 128)
+                    copies.append(
+                        pltpu.make_async_copy(
+                            pieces[lower * RING + k].at[m],
+                            weight.at[pl.ds(lower * half, half), lanes],
+                            arrived.at[(k * RING + m) * 2 + lower],
+                        )
+                    )
+        for copy in copies:
+            copy.start()
+        for copy in copies:
+            copy.wait()
+
+    columns = weight[:, pl.ds(pl.multiple_of(step * block, block), block)]
+    result[:length, :] = dot(mine[...], columns)
+    result[length:, :] = dot(other[...], columns)
+    for index, out in enumerate(outs):
+        pack_of, shift = divmod(index, length // tokens)
+        start = pack_of * length + lax.rem(place[0] + shift, length // tokens) * tokens
+        out[...] = result[pl.ds(pl.multiple_of(start, tokens), tokens), :].astype(out.dtype)
+
+
+def project(place, mine, other, upper, lower, seq_count):
+    length, inner = mine.shape
+    tokens = length // seq_count
+    width = RING * RING * 128
+    steps = 4
+    block = width // steps
+    count = CORES * seq_count
+    return pl.pallas_call(
+        project_kernel,
+        grid_spec=pltpu.PrefetchScalarGridSpec(
+            num_scalar_prefetch=1,
+            grid=(steps,),
+            in_specs=[pl.BlockSpec((length, inner), lambda i, _: (0, 0))] * 2
+            + [pl.BlockSpec(memory_space=pl.ANY)] * (2 * RING),
+            out_specs=[pl.BlockSpec((tokens, block), lambda i, _: (0, i))] * count,
+            scratch_shapes=[
+                pltpu.VMEM((inner, width), BF),
+                pltpu.VMEM((CORES * length, block), F32),
+                pltpu.SemaphoreType.DMA((2 * RING * RING,)),
+            ],
+        ),
+        out_shape=[jax.ShapeDtypeStruct((tokens, width), F32 if k == 0 else BF) for k in range(count)],
+        compiler_params=pltpu.CompilerParams(vmem_limit_bytes=VMEM_LIMIT),
+        name="project",
+    )(place, mine, other, *upper, *lower)
+
+
+def pack_kernel(place, *refs):
+    *sums, residual, gain, main_hot, extra_hot, hidden, out, stacked = refs
     step = pl.program_id(0)
     tokens = residual.shape[0]
     quarter = stacked.shape[1]
+    per_core = len(sums) // CORES
 
     @pl.when(step == 0)
     def _():
-        state = residual[...].astype(F32) + projected[...].astype(F32)
-        hidden[...] = state
-        mean = jnp.mean(state * state, axis=-1, keepdims=True)
-        normed = (state / jnp.sqrt(mean + 1e-06) * gain[...]).astype(BF)
+        total = jnp.zeros((tokens, 128), F32)
+        for core in range(CORES):
+            parts = sums[core * per_core : (core + 1) * per_core]
+            for chip in range(RING * RING):
+                value = parts[0][:, chip * 128 : (chip + 1) * 128].astype(F32)
+                for part in parts[1:]:
+                    value += part[:, chip * 128 : (chip + 1) * 128].astype(F32)
+                shard = chip * CORES + lax.rem(place[3] + core, CORES)
+                lanes = pl.ds(pl.multiple_of(shard * 128, 128), 128)
+                state = residual[:, lanes].astype(F32) + value
+                hidden[:, lanes] = state
+                total += state * state
+        mean = jnp.sum(total, axis=-1, keepdims=True) * (1.0 / hidden.shape[1])
+        root_mean = jnp.sqrt(mean + 1e-06)
         for c in range(QUARTERS):
-            stacked[c * tokens : (c + 1) * tokens, :] = normed[:, c * quarter : (c + 1) * quarter]
+            lanes = slice(c * quarter, (c + 1) * quarter)
+            stacked[c * tokens : (c + 1) * tokens, :] = (hidden[:, lanes] / root_mean * gain[:, lanes]).astype(BF)
 
     @pl.when(step < QUARTERS)
     def _():
@@ -62,30 +165,27 @@
         out[...] = dot(extra_hot[...], stacked[...]).astype(BF)
 
 
-def pack(projected, residual, gain, main_hot, extra_hot):
+def pack(place, sums, residual, gain, main_hot, extra_hot):
     tokens, width = residual.shape
     quarter = width // QUARTERS
     slots = main_hot.shape[0]
-    whole = lambda shape: pl.BlockSpec(shape, lambda i: (0, 0))
+    whole = lambda shape: pl.BlockSpec(shape, lambda i, _: (0, 0))
     return pl.pallas_call(
         pack_kernel,
-        grid=(QUARTERS + 1,),
-        in_specs=[
-            whole((tokens, width)),
-            whole((tokens, width)),
-            whole((1, width)),
-            whole(main_hot.shape),
-            whole(extra_hot.shape),
-        ],
-        out_specs=[whole((tokens, width)), pl.BlockSpec((slots, quarter), lambda i: (0, i))],
+        grid_spec=pltpu.PrefetchScalarGridSpec(
+            num_scalar_prefetch=1,
+            grid=(QUARTERS + 1,),
+            in_specs=[whole(a.shape) for a in (*sums, residual, gain, main_hot, extra_hot)],
+            out_specs=[whole((tokens, width)), pl.BlockSpec((slots, quarter), lambda i, _: (0, i))],
+            scratch_shapes=[pltpu.VMEM((QUARTERS * tokens, quarter), BF)],
+        ),
         out_shape=[
             jax.ShapeDtypeStruct((tokens, width), F32),
             jax.ShapeDtypeStruct((slots, width + quarter), BF),
         ],
-        scratch_shapes=[pltpu.VMEM((QUARTERS * tokens, quarter), BF)],
         compiler_params=pltpu.CompilerParams(vmem_limit_bytes=VMEM_LIMIT),
         name="norm_pack",
-    )(projected, residual, gain, main_hot, extra_hot)
+    )(place, *sums, residual, gain, main_hot, extra_hot)
 
 
 def regroup_matrix(transposed):
@@ -264,7 +364,7 @@
     return main_hot, extra_hot, split_in_two(gates_main), split_in_two(gates_extra), keys_main, keys_extra
 
 
-def shards(
+def layer(
     queries,
     rotated_keys,
     projected_values,
@@ -281,11 +381,16 @@
     seq_count = lax.axis_size("seq")
     experts = seq_count * lax.axis_size("exp")
     tokens, width = residual.shape[1:]
-    full_rows = lax.all_gather(out_weight, "exp", axis=1, tiled=True)
+    along_x, along_z = lambda d: exp_shift(0, d), lambda d: exp_shift(d, 0)
+    half = out_weight.shape[0] // 2
+    upper = gather_line(out_weight[:half], along_x)
+    lower = gather_line(out_weight[half:], along_z)
 
     by_head = lambda a: a[0].reshape(tokens, seq_count, -1)
     heads = jnp.concatenate([by_head(queries), by_head(rotated_keys), by_head(projected_values)], axis=2)
     heads = lax.all_to_all(heads.transpose(1, 0, 2), "seq", split_axis=0, concat_axis=0, tiled=True)
+    heads, upper, lower = lax.optimization_barrier((heads, upper, lower))
+    upper, lower = gather_plane(upper, along_z), gather_plane(lower, along_x)
     heads = heads.reshape(seq_count * tokens, -1)
     q_width = width // seq_count
     attended = attend_heads(
@@ -294,11 +399,21 @@
         heads[:, q_width + HEAD_SIZE :],
         doc_ids[0],
     )
-    partial = dot(attended, full_rows).astype(BF)
-    projected = lax.psum_scatter(partial, "seq", scatter_dimension=0, tiled=True)
+    other = lax.ppermute(attended, "exp", exp_shift(0, 0, 1))
+    seq, exp = lax.axis_index("seq"), lax.axis_index("exp")
+    place = jnp.stack([seq, exp // (RING * CORES), exp // CORES % RING, exp % CORES]).astype(jnp.int32)
+    sums = list(project(place, attended, other, upper, lower, seq_count))
+    for index in range(1, len(sums)):
+        core, shift = divmod(index, seq_count)
+        around = [
+            (s * RING * RING * CORES + a, (s + shift) % seq_count * RING * RING * CORES + b)
+            for s in range(seq_count)
+            for a, b in exp_shift(0, 0, core)
+        ]
+        sums[index] = lax.ppermute(sums[index], ("seq", "exp"), around)
 
     main_hot, extra_hot, gates_main, gates_extra, keys_main, keys_extra = routing(routes[0], gate_vals[0], experts)
-    hidden, outgoing = pack(projected, residual[0], norm_gain[None, :], main_hot, extra_hot)
+    hidden, outgoing = pack(place, sums, residual[0], norm_gain[None, :], main_hot, extra_hot)
 
     def exchange(slots):
         blocks = slots.reshape(experts, MAIN, slots.shape[1])
@@ -328,4 +443,4 @@
         P(("seq", "exp"), None, None),
     )
     out_specs = (P("exp", "seq", None), P("exp", "seq", None))
-    return jax.shard_map(shards, mesh=mesh, in_specs=in_specs, out_specs=out_specs, check_vma=False)
+    return jax.shard_map(layer, mesh=mesh, in_specs=in_specs, out_specs=out_specs, check_vma=False)

time: 468 us -> 468 us (level)
  starting transfers between devices: 12.3 us -> 50.9 us
  waiting for transfers between devices: 210 us -> 181 us
  Pallas kernels: 60.8 us -> 74.7 us
  between operations: 14.3 us -> 1.04 us
  matrix products: 19.6 us -> 11.8 us
    ppermute x0 -> x20, waiting for transfers between devices: none -> 54.6 us  [the longest x7 30.5 us: layer(): sums[index] = lax.ppermute(sums[index], ('seq', 'exp'), around)]
    reduce_scatter x1 -> x0, waiting for transfers between devices: 42.6 us -> none  [shards(): lax.psum_scatter(partial, 'seq', scatter_dimension=0, tiled=True)]
    ppermute x0 -> x20, starting transfers between devices: none -> 38.6 us  [the longest x7 15.9 us: layer(): sums[index] = lax.ppermute(sums[index], ('seq', 'exp'), around)]
    all_gather x1 -> x0, waiting for transfers between devices: 25.8 us -> none  [shards(): full_rows = lax.all_gather(out_weight, 'exp', axis=1, tiled=True)]
    all_to_all x1, waiting for transfers between devices: 15.5 us -> 0.99 us  [layer(): lax.all_to_all(heads.transpose(1, 0, 2), 'seq', split_axis=0, concat_axis...]
    pallas_call x1 -> x2, Pallas kernels: 10.3 us -> 24.2 us  [the longest x1 12.7 us: pack(): pl.pallas_call(pack_kernel, grid_spec=pltpu.PrefetchScalarGridSpec(num_sc...]
    dot_general x2 -> x1, matrix products: 9.63 us -> 0.14 us  [dot(): return jnp.dot(a, b, preferred_element_type=F32)]
  transfers between devices with their start and end apart: 4 -> 22, of which waited for: 4 -> 13; matrix products, arithmetic and copies ran while one was open for 6% -> 5% of each run, Pallas kernels for 0% -> 0%
where the time goes in v2:
time: 468 us; the launch traced here: 464 us
  waiting for transfers between devices  181 us (39%)
  blocking collectives  128 us (27%)
  Pallas kernels  74.7 us (16%)
  starting transfers between devices  50.9 us (11%)
  matrix products  11.8 us (3%)
  other arithmetic  10.3 us (2%)
  local copies, waits for them, and re-layouts  7.06 us (2%)
    all_to_all x1, blocking collectives, exchange(): lax.all_to_all(blocks, ('seq', 'exp'), split_axis=0, concat_axis=0, tiled...  128 us
    all_to_all x1, waiting for transfers between devices, exchange(): lax.all_to_all(blocks, ('seq', 'exp'), split_axis=0, concat_axis=0, tiled...  125 us
    pallas_call x1, Pallas kernels, run_expert(): pl.pallas_call(expert_kernel, grid=(2 * QUARTERS + 1,), in_specs=[pl.Bloc...  34.5 us
    ppermute x7, waiting for transfers between devices, layer(): sums[index] = lax.ppermute(sums[index], ('seq', 'exp'), around)  30.5 us
    ppermute x6, waiting for transfers between devices, gather_plane(): gathered.append(lax.ppermute(line, 'exp', shifts(d)))  21.2 us
    pallas_call x1, Pallas kernels, combine(): pl.pallas_call(combine_kernel, grid=(QUARTERS,), in_specs=[part((slots, q...  16 us
    ppermute x7, starting transfers between devices, layer(): sums[index] = lax.ppermute(sums[index], ('seq', 'exp'), around)  15.9 us
    pallas_call x1, Pallas kernels, pack(): pl.pallas_call(pack_kernel, grid_spec=pltpu.PrefetchScalarGridSpec(num_sc...  12.7 us
  transfers between devices with their start and end apart: 22, of which 13 were waited for; matrix products, arithmetic and copies ran while one was open for 5% of the time, Pallas kernels for 0%

profile of v2, /device:TPU:10, one launch (start us, length us, event | category | flops | bytes accessed | tf_op | source)
XLA Modules:
  0.0 464.5 jit_solution(13229417818943613070)
XLA Ops:
  4.2 4.9 %all-to-all-start = ((bf16[4,128,1280]{2,1,0:T(8,128)(2,1)}), bf16[4,128,1280]{2,1,0:T(8,128)(2,1)S(1)}, u32[]{:S(2)}, u32[]{:S(2)}) async-start(bf16[4,128,1280]{2,1,0:T(8,128)(2,1)} %maximum_bitcast_fusion), calls=%async_computation | async-start | bytes 2621440 | tf_op jit(solution)/shard_map/all_to_all | solution.py:391
  11.9 2.2 collective-permute-start.2
  14.0 1.9 collective-permute-start.3
  16.0 3.6 collective-permute-start.4
  29.6 7.6 %fusion.20 = (f32[8,512]{1,0:T(8,128)S(1)}, f32[8,512,512]{1,2,0:T(8,128)}) fusion(pred[512,512]{0,1:T(8,128)(4,1)} %fusion.9, bf16[512,8,128]{0,2,1:T(8,128)(2,1)} %bitcast.92, bf16[512,1280]{1,0:T(8,128)(2,1)S(1)} %bitcast.84), kind=kOutput, calls=%fused_computation.55 | convolution fusion | flops 545260032 | bytes 9846784 | tf_op jit(solution)/shard_map/sub | solution.py:37
  37.2 4.1 fusion.6
  42.0 2.2 collective-permute-start.12
  46.2 3.6 collective-permute-start.8
  51.8 4.5 collective-permute-done.12.rest_7_
  56.3 4.2 collective-permute-done.7.rest_1_
  60.5 12.5 %collective-permute-done.8.rest_2_ = bf16[4,512,128]{2,1,0:T(8,128)(2,1)} collective-permute-done((bf16[4,512,128]{2,1,0:T(8,128)(2,1)S(1)}, bf16[4,512,128]{2,1,0:T(8,128)(2,1)}, u32[]{:S(2)}, u32[]{:S(2)}) %collective-permute-start.8) | collective-permute-done | bytes 524320 | tf_op jit(solution)/shard_map/ppermute | solution.py:62
  73.1 11.5 %project.1 = (f32[128,2048]{1,0:T(8,128)}, bf16[128,2048]{1,0:T(8,128)(2,1)}, bf16[128,2048]{1,0:T(8,128)(2,1)}, bf16[128,2048]{1,0:T(8,128)(2,1)}, bf16[128,204...) custom-call(s32[4]{0:T(128)} %pad_add_fusion.place, ...), custom_call_target="tpu_custom_call" | custom-call | tf_op jit(solution)/shard_map/project/pallas_call | solution.py:111
  84.8 3.5 collective-permute-start.14
  91.0 8.9 %collective-permute-done.13.refs_1_ = bf16[128,2048]{1,0:T(8,128)(2,1)S(1)} collective-permute-done((bf16[128,2048]{1,0:T(8,128)(2,1)}, bf16[128,2048]{1,0:T(8,128)(2,1)S(1)}, u32[]{:S(2)}, u32[]{:S(2)}) %collective-permute-start.13) | collective-permute-done | bytes 524320 | tf_op jit(solution)/shard_map/ppermute | solution.py:413
  101.5 9.9 %collective-permute-start.19 = (bf16[128,2048]{1,0:T(8,128)(2,1)}, bf16[128,2048]{1,0:T(8,128)(2,1)}, u32[]{:S(2)}, u32[]{:S(2)}) collective-permute-start(bf16[128,2048]{1,0:T(8,128)(2,1)} %get-tuple-element.27), channel_id=1, source_target_pairs={{0,97},{1,96},{2,99},{3,98},{4,101},{5,100},{6,103},{7,102},{8,105... | collective-permute-start | bytes 1572872 | tf_op jit(solution)/shard_map/ppermute | solution.py:413
  113.6 5.3 %collective-permute-done.17.refs_5_ = bf16[128,2048]{1,0:T(8,128)(2,1)S(1)} collective-permute-done((bf16[128,2048]{1,0:T(8,128)(2,1)}, bf16[128,2048]{1,0:T(8,128)(2,1)S(1)}, u32[]{:S(2)}, u32[]{:S(2)}) %collective-permute-start.17) | collective-permute-done | bytes 524320 | tf_op jit(solution)/shard_map/ppermute | solution.py:413
  119.7 13.9 %collective-permute-done.19.refs_7_ = bf16[128,2048]{1,0:T(8,128)(2,1)} collective-permute-done((bf16[128,2048]{1,0:T(8,128)(2,1)}, bf16[128,2048]{1,0:T(8,128)(2,1)}, u32[]{:S(2)}, u32[]{:S(2)}) %collective-permute-start.19) | collective-permute-done | bytes 524320 | tf_op jit(solution)/shard_map/ppermute | solution.py:413
  133.6 12.7 %norm_pack.1 = (f32[128,4096]{1,0:T(8,128)}, bf16[1024,5120]{1,0:T(8,128)(2,1)}) custom-call(s32[4]{0:T(128)} %pad_add_fusion.place, f32[128,2048]{1,0:T(8,128)} %get-tuple-element.20.refs_0_, bf16[128,2048]{1,0:T(8,128)(2,1)} %copy-done.3, bf16[128,2048]{1,0:T(8,128)(2,1)} %copy-done.4, bf16[128,2048]{1,0:T(8,128)(2,1)} %copy-done.5, ...), custom_call_target="tpu_custom_call" | custom-call | tf_op jit(solution)/shard_map/norm_pack/pallas_call | solution.py:173
  146.3 127.6 %all_to_all.15 = bf16[128,8,5120]{2,1,0:T(8,128)(2,1)} all-to-all(bf16[128,8,5120]{2,1,0:T(8,128)(2,1)} %bitcast.81), channel_id=1, replica_groups=mesh['seq'=4,'exp'=32] {'seq','exp'}, dimensions={0} | all-to-all | bytes 20971520 | tf_op jit(solution)/shard_map/all_to_all | solution.py:420
  273.9 34.5 %experts.1 = bf16[1024,5120]{1,0:T(8,128)(2,1)} custom-call(bf16[1024,5120]{1,0:T(8,128)(2,1)} %bitcast.77, bf16[1024,5120]{1,0:T(8,128)(2,1)} %bitcast.78, bf16[4096,1536]{1,0:T(8,128)(2,1)} %bitcast.80, bf16[768,4096]{1,0:T(8,128)(2,1)} %bitcast.82), custom_call_target="tpu_custom_call" | custom-call | tf_op jit(solution)/shard_map/experts/pallas_call | solution.py:251
  308.4 7.3 %all-to-all-start.2 = ((bf16[128,8,5120]{2,1,0:T(8,128)(2,1)}), bf16[128,8,5120]{2,1,0:T(8,128)(2,1)}, u32[]{:S(2)}, u32[]{:S(2)}) async-start(bf16[128,8,5120]{2,1,0:T(8,128)(2,1)} %bitcast.79), calls=%async_computation.2 | async-start | bytes 20971520 | tf_op jit(solution)/shard_map/all_to_all | solution.py:420
  318.4 2.4 select_reduce_fusion
  321.5 125.5 %all-to-all-done.2 = bf16[128,8,5120]{2,1,0:T(8,128)(2,1)} async-done(((bf16[128,8,5120]{2,1,0:T(8,128)(2,1)}), bf16[128,8,5120]{2,1,0:T(8,128)(2,1)}, u32[]{:S(2)}, u32[]{:S(2)}) %all-to-all-start.2) | async-done | bytes 10485792 | tf_op jit(solution)/shard_map/all_to_all | solution.py:420
  447.0 16.0 %combine.1 = (bf16[128,4096]{1,0:T(8,128)(2,1)}, f32[128,8]{1,0:T(8,128)}) custom-call(bf16[1024,5120]{1,0:T(8,128)(2,1)} %bitcast.33.main.extra, bf16[1024,5120]{1,0:T(8,128)(2,1)} %bitcast.33.main.extra, f32[128,4096]{1,0:T(8,128)} %get-tuple-element.29.hidden, bf16[128,4096]{1,0:T(8,128)(2,1)} %bitcast.90, ...), custom_call_target="tpu_custom_call" | custom-call | tf_op jit(solution)/shard_map/combine/pallas_call | solution.py:316
  (102 shorter events, 33.1 us)
Async XLA Ops:
  4.2 21.4 %all-to-all-start = ((bf16[4,128,1280]{2,1,0:T(8,128)(2,1)}), bf16[4,128,1280]{2,1,0:T(8,128)(2,1)S(1)}, u32[]{:S(2)}, u32[]{:S(2)}) async-start(bf16[4,128,1280]{2,1,0:T(8,128)(2,1)} %maximum_bitcast_fusion), calls=%async_computation | async-start | bytes 2621440 | tf_op jit(solution)/shard_map/all_to_all | solution.py:391
  9.2 10.3 %collective-permute-start = (bf16[512,128]{1,0:T(8,128)(2,1)S(1)}, bf16[512,128]{1,0:T(8,128)(2,1)S(1)}, u32[]{:S(2)}, u32[]{:S(2)}) collective-permute-start(bf16[512,128]{1,0:T(8,128)(2,1)S(1)} %get-tuple-element.45), channel_id=1, source_target_pairs={{0,2},{1,3},{2,4},{3,5},{4,6},{5,7},{6,0},{7,1},{8,10},{9,11},{10,... | collective-permute-start | bytes 393224 | tf_op jit(solution)/shard_map/ppermute | solution.py:56
  10.8 10.7 %collective-permute-start.1 = (bf16[512,128]{1,0:T(8,128)(2,1)S(1)}, bf16[512,128]{1,0:T(8,128)(2,1)S(1)}, u32[]{:S(2)}, u32[]{:S(2)}) collective-permute-start(bf16[512,128]{1,0:T(8,128)(2,1)S(1)} %get-tuple-element.45), channel_id=1, source_target_pairs={{0,4},{1,5},{2,6},{3,7},{4,0},{5,1},{6,2},{7,3},{8,12},{9,13},{10,... | collective-permute-start | bytes 393224 | tf_op jit(solution)/shard_map/ppermute | solution.py:56
  11.9 9.6 %collective-permute-start.2 = (bf16[512,128]{1,0:T(8,128)(2,1)S(1)}, bf16[512,128]{1,0:T(8,128)(2,1)S(1)}, u32[]{:S(2)}, u32[]{:S(2)}) collective-permute-start(bf16[512,128]{1,0:T(8,128)(2,1)S(1)} %get-tuple-element.45), channel_id=1, source_target_pairs={{0,6},{1,7},{2,0},{3,1},{4,2},{5,3},{6,4},{7,5},{8,14},{9,15},{10,... | collective-permute-start | bytes 393224 | tf_op jit(solution)/shard_map/ppermute | solution.py:56
  14.0 8.4 %collective-permute-start.3 = (bf16[512,128]{1,0:T(8,128)(2,1)S(1)}, bf16[512,128]{1,0:T(8,128)(2,1)S(1)}, u32[]{:S(2)}, u32[]{:S(2)}) collective-permute-start(bf16[512,128]{1,0:T(8,128)(2,1)S(1)} %get-tuple-element.44), channel_id=1, source_target_pairs={{0,8},{1,9},{2,10},{3,11},{4,12},{5,13},{6,14},{7,15},{8,16},{9,17... | collective-permute-start | bytes 393224 | tf_op jit(solution)/shard_map/ppermute | solution.py:56
  16.0 8.2 %collective-permute-start.4 = (bf16[512,128]{1,0:T(8,128)(2,1)S(1)}, bf16[512,128]{1,0:T(8,128)(2,1)S(1)}, u32[]{:S(2)}, u32[]{:S(2)}) collective-permute-start(bf16[512,128]{1,0:T(8,128)(2,1)S(1)} %get-tuple-element.44), channel_id=1, source_target_pairs={{0,16},{1,17},{2,18},{3,19},{4,20},{5,21},{6,22},{7,23},{8,24},{9,... | collective-permute-start | bytes 393224 | tf_op jit(solution)/shard_map/ppermute | solution.py:56
  19.5 5.0 %collective-permute-start.5 = (bf16[512,128]{1,0:T(8,128)(2,1)S(1)}, bf16[512,128]{1,0:T(8,128)(2,1)S(1)}, u32[]{:S(2)}, u32[]{:S(2)}) collective-permute-start(bf16[512,128]{1,0:T(8,128)(2,1)S(1)} %get-tuple-element.44), channel_id=1, source_target_pairs={{0,24},{1,25},{2,26},{3,27},{4,28},{5,29},{6,30},{7,31},{8,0},{9,1... | collective-permute-start | bytes 393224 | tf_op jit(solution)/shard_map/ppermute | solution.py:56
  25.6 20.6 %collective-permute-start.10 = (bf16[4,512,128]{2,1,0:T(8,128)(2,1)S(1)}, bf16[4,512,128]{2,1,0:T(8,128)(2,1)}, u32[]{:S(2)}, u32[]{:S(2)}) collective-permute-start(bf16[4,512,128]{2,1,0:T(8,128)(2,1)S(1)} %pad_maximum_fusion.1.rest_4_), channel_id=1, source_target_pairs={{0,2},{1,3},{2,4},{3,5},{4,6},{5,7},{6,0},{7,1},{8,10},{9,11},{10,... | collective-permute-start | bytes 1572872 | tf_op jit(solution)/shard_map/ppermute | solution.py:62
  27.1 22.7 %collective-permute-start.11 = (bf16[4,512,128]{2,1,0:T(8,128)(2,1)S(1)}, bf16[4,512,128]{2,1,0:T(8,128)(2,1)}, u32[]{:S(2)}, u32[]{:S(2)}) collective-permute-start(bf16[4,512,128]{2,1,0:T(8,128)(2,1)S(1)} %pad_maximum_fusion.1.rest_4_), channel_id=1, source_target_pairs={{0,4},{1,5},{2,6},{3,7},{4,0},{5,1},{6,2},{7,3},{8,12},{9,13},{10,... | collective-permute-start | bytes 1572872 | tf_op jit(solution)/shard_map/ppermute | solution.py:62
  41.9 31.1 %collective-permute-start.6 = (bf16[512,1024]{1,0:T(8,128)(2,1)S(1)}, bf16[512,1024]{1,0:T(8,128)(2,1)}, u32[]{:S(2)}, u32[]{:S(2)}) collective-permute-start(bf16[512,1024]{1,0:T(8,128)(2,1)S(1)} %copy.63.mine), channel_id=1, source_target_pairs={{0,1},{1,0},{2,3},{3,2},{4,5},{5,4},{6,7},{7,6},{8,9},{9,8},{10,11... | collective-permute-start | bytes 3145736 | tf_op jit(solution)/shard_map/ppermute | solution.py:402
  42.0 14.3 %collective-permute-start.12 = (bf16[4,512,128]{2,1,0:T(8,128)(2,1)S(1)}, bf16[4,512,128]{2,1,0:T(8,128)(2,1)S(1)}, u32[]{:S(2)}, u32[]{:S(2)}) collective-permute-start(bf16[4,512,128]{2,1,0:T(8,128)(2,1)S(1)} %pad_maximum_fusion.1.rest_4_), channel_id=1, source_target_pairs={{0,6},{1,7},{2,0},{3,1},{4,2},{5,3},{6,4},{7,5},{8,14},{9,15},{10,... | collective-permute-start | bytes 1572872 | tf_op jit(solution)/shard_map/ppermute | solution.py:62
  44.2 16.3 %collective-permute-start.7 = (bf16[4,512,128]{2,1,0:T(8,128)(2,1)S(1)}, bf16[4,512,128]{2,1,0:T(8,128)(2,1)S(1)}, u32[]{:S(2)}, u32[]{:S(2)}) collective-permute-start(bf16[4,512,128]{2,1,0:T(8,128)(2,1)S(1)} %pad_maximum_fusion.rest_0_), channel_id=1, source_target_pairs={{0,8},{1,9},{2,10},{3,11},{4,12},{5,13},{6,14},{7,15},{8,16},{9,17... | collective-permute-start | bytes 1572872 | tf_op jit(solution)/shard_map/ppermute | solution.py:62
  46.2 26.9 %collective-permute-start.8 = (bf16[4,512,128]{2,1,0:T(8,128)(2,1)S(1)}, bf16[4,512,128]{2,1,0:T(8,128)(2,1)}, u32[]{:S(2)}, u32[]{:S(2)}) collective-permute-start(bf16[4,512,128]{2,1,0:T(8,128)(2,1)S(1)} %pad_maximum_fusion.rest_0_), channel_id=1, source_target_pairs={{0,16},{1,17},{2,18},{3,19},{4,20},{5,21},{6,22},{7,23},{8,24},{9,... | collective-permute-start | bytes 1572872 | tf_op jit(solution)/shard_map/ppermute | solution.py:62
  49.8 23.3 %collective-permute-start.9 = (bf16[4,512,128]{2,1,0:T(8,128)(2,1)S(1)}, bf16[4,512,128]{2,1,0:T(8,128)(2,1)}, u32[]{:S(2)}, u32[]{:S(2)}) collective-permute-start(bf16[4,512,128]{2,1,0:T(8,128)(2,1)S(1)} %pad_maximum_fusion.rest_0_), channel_id=1, source_target_pairs={{0,24},{1,25},{2,26},{3,27},{4,28},{5,29},{6,30},{7,31},{8,0},{9,1... | collective-permute-start | bytes 1572872 | tf_op jit(solution)/shard_map/ppermute | solution.py:62
  84.6 15.3 %collective-permute-start.13 = (bf16[128,2048]{1,0:T(8,128)(2,1)}, bf16[128,2048]{1,0:T(8,128)(2,1)S(1)}, u32[]{:S(2)}, u32[]{:S(2)}) collective-permute-start(bf16[128,2048]{1,0:T(8,128)(2,1)} %get-tuple-element.21), channel_id=1, source_target_pairs={{0,32},{1,33},{2,34},{3,35},{4,36},{5,37},{6,38},{7,39},{8,40},{9,... | collective-permute-start | bytes 1572872 | tf_op jit(solution)/shard_map/ppermute | solution.py:413
  84.8 16.6 %collective-permute-start.14 = (bf16[128,2048]{1,0:T(8,128)(2,1)}, bf16[128,2048]{1,0:T(8,128)(2,1)S(1)}, u32[]{:S(2)}, u32[]{:S(2)}) collective-permute-start(bf16[128,2048]{1,0:T(8,128)(2,1)} %get-tuple-element.22), channel_id=1, source_target_pairs={{0,64},{1,65},{2,66},{3,67},{4,68},{5,69},{6,70},{7,71},{8,72},{9,... | collective-permute-start | bytes 1572872 | tf_op jit(solution)/shard_map/ppermute | solution.py:413
  88.8 24.9 %collective-permute-start.15 = (bf16[128,2048]{1,0:T(8,128)(2,1)}, bf16[128,2048]{1,0:T(8,128)(2,1)S(1)}, u32[]{:S(2)}, u32[]{:S(2)}) collective-permute-start(bf16[128,2048]{1,0:T(8,128)(2,1)} %get-tuple-element.23), channel_id=1, source_target_pairs={{0,96},{1,97},{2,98},{3,99},{4,100},{5,101},{6,102},{7,103},{8,104... | collective-permute-start | bytes 1572872 | tf_op jit(solution)/shard_map/ppermute | solution.py:413
  89.4 24.2 %collective-permute-start.16 = (bf16[128,2048]{1,0:T(8,128)(2,1)}, bf16[128,2048]{1,0:T(8,128)(2,1)S(1)}, u32[]{:S(2)}, u32[]{:S(2)}) collective-permute-start(bf16[128,2048]{1,0:T(8,128)(2,1)} %get-tuple-element.24), channel_id=1, source_target_pairs={{0,1},{1,0},{2,3},{3,2},{4,5},{5,4},{6,7},{7,6},{8,9},{9,8},{10,11... | collective-permute-start | bytes 1572872 | tf_op jit(solution)/shard_map/ppermute | solution.py:413
  89.4 29.6 %collective-permute-start.17 = (bf16[128,2048]{1,0:T(8,128)(2,1)}, bf16[128,2048]{1,0:T(8,128)(2,1)S(1)}, u32[]{:S(2)}, u32[]{:S(2)}) collective-permute-start(bf16[128,2048]{1,0:T(8,128)(2,1)} %get-tuple-element.25), channel_id=1, source_target_pairs={{0,33},{1,32},{2,35},{3,34},{4,37},{5,36},{6,39},{7,38},{8,41},{9,... | collective-permute-start | bytes 1572872 | tf_op jit(solution)/shard_map/ppermute | solution.py:413
  99.8 33.8 %copy-start.3 = (bf16[128,2048]{1,0:T(8,128)(2,1)}, bf16[128,2048]{1,0:T(8,128)(2,1)S(1)}, u32[]{:S(2)}) copy-start(bf16[128,2048]{1,0:T(8,128)(2,1)S(1)} %collective-permute-done.13.refs_1_) | copy-start | bytes 1572868
  99.8 19.8 %collective-permute-start.18 = (bf16[128,2048]{1,0:T(8,128)(2,1)}, bf16[128,2048]{1,0:T(8,128)(2,1)}, u32[]{:S(2)}, u32[]{:S(2)}) collective-permute-start(bf16[128,2048]{1,0:T(8,128)(2,1)} %get-tuple-element.26), channel_id=1, source_target_pairs={{0,65},{1,64},{2,67},{3,66},{4,69},{5,68},{6,71},{7,70},{8,73},{9,... | collective-permute-start | bytes 1572872 | tf_op jit(solution)/shard_map/ppermute | solution.py:413
  101.5 32.1 %copy-start.4 = (bf16[128,2048]{1,0:T(8,128)(2,1)}, bf16[128,2048]{1,0:T(8,128)(2,1)S(1)}, u32[]{:S(2)}) copy-start(bf16[128,2048]{1,0:T(8,128)(2,1)S(1)} %collective-permute-done.14.refs_2_) | copy-start | bytes 1572868
  101.5 32.1 %collective-permute-start.19 = (bf16[128,2048]{1,0:T(8,128)(2,1)}, bf16[128,2048]{1,0:T(8,128)(2,1)}, u32[]{:S(2)}, u32[]{:S(2)}) collective-permute-start(bf16[128,2048]{1,0:T(8,128)(2,1)} %get-tuple-element.27), channel_id=1, source_target_pairs={{0,97},{1,96},{2,99},{3,98},{4,101},{5,100},{6,103},{7,102},{8,105... | collective-permute-start | bytes 1572872 | tf_op jit(solution)/shard_map/ppermute | solution.py:413
  308.4 138.6 %all-to-all-start.2 = ((bf16[128,8,5120]{2,1,0:T(8,128)(2,1)}), bf16[128,8,5120]{2,1,0:T(8,128)(2,1)}, u32[]{:S(2)}, u32[]{:S(2)}) async-start(bf16[128,8,5120]{2,1,0:T(8,128)(2,1)} %bitcast.79), calls=%async_computation.2 | async-start | bytes 20971520 | tf_op jit(solution)/shard_map/all_to_all | solution.py:420
  (14 other events, 211.1 us)

commit v3 on v2

--- a/solution.py
+++ b/solution.py
@@ -150,10 +150,10 @@
                 hidden[:, lanes] = state
                 total += state * state
         mean = jnp.sum(total, axis=-1, keepdims=True) * (1.0 / hidden.shape[1])
-        root_mean = jnp.sqrt(mean + 1e-06)
+        scale = 1.0 / jnp.sqrt(mean + 1e-06)
         for c in range(QUARTERS):
             lanes = slice(c * quarter, (c + 1) * quarter)
-            stacked[c * tokens : (c + 1) * tokens, :] = (hidden[:, lanes] / root_mean * gain[:, lanes]).astype(BF)
+            stacked[c * tokens : (c + 1) * tokens, :] = (hidden[:, lanes] * scale * gain[:, lanes]).astype(BF)
 
     @pl.when(step < QUARTERS)
     def _():
@@ -197,141 +197,187 @@
     return (source == plain).astype(F32).astype(BF)
 
 
-def expert_kernel(main, extra, w_in, w_down, out, acc, act, parts):
-    step = pl.program_id(0)
-    slots = main.shape[0]
+def regroup(extra, parts):
+    size = 32 * QUARTERS * EXTRA
+    per = 32 * EXTRA
+    swap = regroup_matrix(False)
+    for g in range(extra.shape[0] // size):
+        rows = dot(swap, extra[g * size : (g + 1) * size, :]).astype(BF)
+        for c in range(QUARTERS):
+            parts[c, g * per : (g + 1) * per, :] = rows[c * per : (c + 1) * per, :]
+
+
+def ungroup(parts, out):
+    size = 32 * QUARTERS * EXTRA
+    per = 32 * EXTRA
+    swap = regroup_matrix(True)
+    for g in range(out.shape[0] // size):
+        rows = jnp.concatenate([parts[c, g * per : (g + 1) * per, :] for c in range(QUARTERS)], axis=0)
+        out[g * size : (g + 1) * size, :] = dot(swap, rows).astype(BF)
+
+
+def up_step(step, rows, w_in, acc, act):
     hidden = act.shape[1]
-    extras = parts.shape[1]
-    groups = slots // 256
-    per = extras // groups
-
-    @pl.when(step == 0)
-    def _():
-        swap = regroup_matrix(False)
-        for g in range(groups):
-            rows = dot(swap, extra[g * 256 : (g + 1) * 256, :]).astype(BF)
-            for c in range(QUARTERS):
-                parts[c, g * per : (g + 1) * per, :] = rows[c * per : (c + 1) * per, :]
-
-    @pl.when(step == 0)
-    def _():
-        acc[:slots, :] = dot(main[...], w_in[...])
-        acc[slots:, :] = dot(parts[0], w_in[...])
-
-    @pl.when((step > 0) & (step < QUARTERS))
-    def _():
-        acc[:slots, :] += dot(main[...], w_in[...])
-        acc[slots:, :] += dot(parts[step], w_in[...])
+
+    @pl.when(step == 0)
+    def _():
+        @pl.loop(0, acc.shape[0] // 64)
+        def _(r):
+            acc[pl.ds(pl.multiple_of(r * 64, 64), 64), :] = jnp.zeros((64, acc.shape[1]), F32)
+
+    acc[...] += dot(rows, w_in[...])
 
     @pl.when(step == QUARTERS - 1)
     def _():
         gate = acc[:, :hidden]
         act[...] = (gate / (1.0 + jnp.exp(-gate)) * acc[:, hidden:]).astype(BF)
 
-    @pl.when((step >= QUARTERS) & (step < 2 * QUARTERS))
-    def _():
-        out[...] = dot(act[:slots, :], w_down[...]).astype(BF)
-        parts[step - QUARTERS] = dot(act[slots:, :], w_down[...]).astype(BF)
-
-    @pl.when(step == 2 * QUARTERS)
-    def _():
-        swap = regroup_matrix(True)
-        for g in range(groups):
-            rows = jnp.concatenate([parts[c, g * per : (g + 1) * per, :] for c in range(QUARTERS)], axis=0)
-            out[g * 256 : (g + 1) * 256, :] = dot(swap, rows).astype(BF)
-
-
-def run_expert(incoming, w_in, w_down):
+
+def main_kernel(after, main, w_in, w_down, out, acc, act):
+    step = pl.program_id(0)
+
+    @pl.when(step < QUARTERS)
+    def _():
+        up_step(step, main[...], w_in, acc, act)
+
+    @pl.when(step >= QUARTERS)
+    def _():
+        out[...] = dot(act[...], w_down[...]).astype(BF)
+
+
+def extra_kernel(extra, w_in, w_down, out, acc, act, parts):
+    step = pl.program_id(0)
+
+    @pl.when(step == 0)
+    def _():
+        regroup(extra, parts)
+
+    @pl.when(step < QUARTERS)
+    def _():
+        up_step(step, parts[step], w_in, acc, act)
+
+    @pl.when(step >= QUARTERS)
+    def _():
+        parts[step - QUARTERS] = dot(act[...], w_down[...]).astype(BF)
+
+    @pl.when(step == 2 * QUARTERS - 1)
+    def _():
+        ungroup(parts, out)
+
+
+def run_expert(incoming, w_in, w_down, after=None):
     slots = incoming.shape[0]
     width = w_in.shape[0]
     hidden = w_down.shape[0]
     quarter = width // QUARTERS
-    extras = slots // MAIN * EXTRA
     last = QUARTERS - 1
+    main = after is not None
+    rows = slots if main else slots // MAIN * EXTRA
+    if main:
+        in_specs = [
+            pl.BlockSpec(memory_space=pl.ANY),
+            pl.BlockSpec((slots, quarter), lambda i: (0, jnp.minimum(i, last))),
+        ]
+        out_specs = pl.BlockSpec((slots, quarter), lambda i: (0, jnp.maximum(i - QUARTERS, 0)))
+        out_width, scratch = width, []
+    else:
+        in_specs = [pl.BlockSpec((slots, quarter), lambda i: (0, QUARTERS))]
+        out_specs = pl.BlockSpec((slots, quarter), lambda i: (0, 0))
+        out_width, scratch = quarter, [pltpu.VMEM((QUARTERS, rows, quarter), BF)]
     return pl.pallas_call(
-        expert_kernel,
-        grid=(2 * QUARTERS + 1,),
-        in_specs=[
-            pl.BlockSpec((slots, quarter), lambda i: (0, jnp.minimum(i, last))),
-            pl.BlockSpec((slots, quarter), lambda i: (0, QUARTERS)),
+        main_kernel if main else extra_kernel,
+        grid=(2 * QUARTERS,),
+        in_specs=in_specs
+        + [
             pl.BlockSpec((quarter, 2 * hidden), lambda i: (jnp.minimum(i, last), 0)),
             pl.BlockSpec((hidden, quarter), lambda i: (0, jnp.clip(i - QUARTERS, 0, last))),
         ],
-        out_specs=pl.BlockSpec((slots, quarter), lambda i: (0, jnp.maximum(i - QUARTERS, 0))),
-        out_shape=jax.ShapeDtypeStruct((slots, width + quarter), BF),
-        scratch_shapes=[
-            pltpu.VMEM((slots + extras, 2 * hidden), F32),
-            pltpu.VMEM((slots + extras, hidden), BF),
-            pltpu.VMEM((QUARTERS, extras, quarter), BF),
-        ],
+        out_specs=out_specs,
+        out_shape=jax.ShapeDtypeStruct((slots, out_width), BF),
+        scratch_shapes=[pltpu.VMEM((rows, 2 * hidden), F32), pltpu.VMEM((rows, hidden), BF)] + scratch,
         compiler_params=pltpu.CompilerParams(vmem_limit_bytes=VMEM_LIMIT),
-        name="experts",
-    )(incoming, incoming, w_in, w_down)
-
-
-def combine_kernel(main, extra, hidden, cot, gates_main, gates_extra, keys_main, keys_extra, out, grad, dots_main, dots_extra):
+        name="experts_main" if main else "experts_extra",
+    )(*([after] if main else []), incoming, w_in, w_down)
+
+
+def select_dots(dots, keys):
+    slot = lax.broadcasted_iota(jnp.int32, dots.shape, 1)
+    column = lax.broadcasted_iota(jnp.int32, (dots.shape[0], 128), 1)
+    picked = jnp.zeros((dots.shape[0], 128), F32)
+    for k in range(keys.shape[1]):
+        entry = jnp.sum(jnp.where(slot == keys[:, k : k + 1], dots[...], 0.0), axis=1, keepdims=True)
+        picked = jnp.where(column == k, entry, picked)
+    return picked
+
+
+def combine_step(rows, hidden, cot, gates, out, dots):
     step = pl.program_id(0)
     tokens = hidden.shape[0]
-    slots = main.shape[0]
-    of_quarter = lax.broadcasted_iota(jnp.int32, (1, slots), 1) % (QUARTERS * EXTRA) // EXTRA == step
-    from_main = dot(gates_main[...], main[...])
-    weights = jnp.where(of_quarter, gates_extra[...].astype(F32), 0.0).astype(BF)
-    from_extra = dot(weights, extra[...])
-    mixed = hidden[...] + (from_main[:tokens] + from_main[tokens:] + from_extra[:tokens] + from_extra[tokens:])
-    out[...] = mixed.astype(BF)
-    contract_last = (((1,), (1,)), ((), ()))
-    new_main = lax.dot_general(cot[...], main[...], contract_last, preferred_element_type=F32)
-    new_extra = lax.dot_general(cot[...], extra[...], contract_last, preferred_element_type=F32)
-    new_extra = jnp.where(of_quarter, new_extra, 0.0)
-
-    @pl.when(step == 0)
-    def _():
-        dots_main[...] = new_main
-        dots_extra[...] = new_extra
+    mixed = dot(gates[...], rows)
+    out[...] = (hidden[...] + (mixed[:tokens] + mixed[tokens:])).astype(out.dtype)
+    more = lax.dot_general(cot[...], rows, (((1,), (1,)), ((), ())), preferred_element_type=F32)
+
+    @pl.when(step == 0)
+    def _():
+        dots[...] = more
 
     @pl.when(step > 0)
     def _():
-        dots_main[...] += new_main
-        dots_extra[...] += new_extra
+        dots[...] += more
+
+
+def combine_extra(extra, hidden, cot, gates, keys, out, grad, dots, parts):
+    step = pl.program_id(0)
+
+    @pl.when(step == 0)
+    def _():
+        regroup(extra, parts)
+
+    combine_step(parts[step], hidden, cot, gates, out, dots)
 
     @pl.when(step == QUARTERS - 1)
     def _():
-        slot = lax.broadcasted_iota(jnp.int32, (tokens, slots), 1)
-        extra_slot = slot // (QUARTERS * EXTRA) * EXTRA + slot % EXTRA
-        sums = []
-        for k in range(keys_main.shape[1]):
-            picked = jnp.where(slot == keys_main[:, k : k + 1], dots_main[...], 0.0)
-            picked += jnp.where(extra_slot == keys_extra[:, k : k + 1], dots_extra[...], 0.0)
-            sums.append(jnp.sum(picked, axis=1, keepdims=True))
-        grad[...] = jnp.concatenate(sums, axis=1)
-
-
-def combine(returned, hidden, cot, gates_main, gates_extra, keys_main, keys_extra):
+        grad[...] = select_dots(dots, keys)
+
+
+def combine_main(main, hidden, cot, gates, keys, before, out, grad, dots):
+    combine_step(main[...], hidden, cot, gates, out, dots)
+
+    @pl.when(pl.program_id(0) == QUARTERS - 1)
+    def _():
+        grad[...] = (select_dots(dots, keys) + before[...]).T[: keys.shape[1], :]
+
+
+def combine(returned, hidden, cot, gates, keys, before=None):
     slots = returned.shape[0]
     tokens, width = hidden.shape
     quarter = width // QUARTERS
-    top = keys_main.shape[1]
+    top = keys.shape[1]
+    count = gates.shape[1]
     whole = lambda shape: pl.BlockSpec(shape, lambda i: (0, 0))
     part = lambda shape: pl.BlockSpec(shape, lambda i: (0, i))
+    main = before is not None
+    more = [before] if main else []
+    grad = (top, tokens) if main else (tokens, 128)
     return pl.pallas_call(
-        combine_kernel,
+        combine_main if main else combine_extra,
         grid=(QUARTERS,),
         in_specs=[
-            part((slots, quarter)),
-            pl.BlockSpec((slots, quarter), lambda i: (0, QUARTERS)),
+            part((slots, quarter)) if main else whole((slots, quarter)),
             part((tokens, quarter)),
             part((tokens, quarter)),
-            whole(gates_main.shape),
-            whole(gates_extra.shape),
-            whole(keys_main.shape),
-            whole(keys_extra.shape),
+        ]
+        + [whole(a.shape) for a in (gates, keys, *more)],
+        out_specs=[part((tokens, quarter)), whole(grad)],
+        out_shape=[
+            jax.ShapeDtypeStruct((tokens, width), BF if main else F32),
+            jax.ShapeDtypeStruct(grad, F32),
         ],
-        out_specs=[part((tokens, quarter)), whole((tokens, top))],
-        out_shape=[jax.ShapeDtypeStruct((tokens, width), BF), jax.ShapeDtypeStruct((tokens, top), F32)],
-        scratch_shapes=[pltpu.VMEM((tokens, slots), F32), pltpu.VMEM((tokens, slots), F32)],
+        scratch_shapes=[pltpu.VMEM((tokens, count), F32)]
+        + ([] if main else [pltpu.VMEM((QUARTERS, count, quarter), BF)]),
         compiler_params=pltpu.CompilerParams(vmem_limit_bytes=VMEM_LIMIT),
-        name="combine",
-    )(returned, returned, hidden, cot, gates_main, gates_extra, keys_main, keys_extra)
+        name="combine_main" if main else "combine_extra",
+    )(returned, hidden, cot, gates, keys, *more)
 
 
 def split_in_two(values):
@@ -358,7 +404,8 @@
     extra_hot = extra_hot.reshape(experts * QUARTERS * EXTRA, QUARTERS * tokens)
 
     gates_main = jnp.where(is_main, gate_of[:, :, None], 0.0).reshape(tokens, experts * MAIN)
-    gates_extra = jnp.where(is_extra, gate_of[:, :, None], 0.0).reshape(tokens, experts * QUARTERS * EXTRA)
+    is_extra = rank[:, :, None] == MAIN + jnp.arange(EXTRA, dtype=jnp.int32)
+    gates_extra = jnp.where(is_extra, gate_of[:, :, None], 0.0).reshape(tokens, experts * EXTRA)
     keys_main = jnp.where(pair_rank < MAIN, chosen * MAIN + pair_rank, -1)
     keys_extra = jnp.where(pair_rank >= MAIN, chosen * EXTRA + pair_rank - MAIN, -1)
     return main_hot, extra_hot, split_in_two(gates_main), split_in_two(gates_extra), keys_main, keys_extra
@@ -420,11 +467,15 @@
         blocks = lax.all_to_all(blocks, ("seq", "exp"), split_axis=0, concat_axis=0, tiled=True)
         return blocks.reshape(slots.shape)
 
-    results = run_expert(exchange(outgoing), expert_in[0], expert_down[0])
-    layer_out, gate_grad = combine(
-        exchange(results), hidden, cotangent[0], gates_main, gates_extra, keys_main, keys_extra
-    )
-    return layer_out[None], gate_grad[None]
+    incoming = exchange(outgoing)
+    results = run_expert(incoming, expert_in[0], expert_down[0])
+    returned = exchange(results)
+    main_results = run_expert(incoming, expert_in[0], expert_down[0], after=results)
+    cot = cotangent[0]
+    hidden, grad = combine(returned, hidden, cot, gates_extra, keys_extra)
+    returned = exchange(main_results)
+    layer_out, gate_grad = combine(returned, hidden, cot, gates_main, keys_main, grad)
+    return layer_out[None], gate_grad.T[None]
 
 
 def solution(mesh):

time: 468 us -> 454 us (0.970)
  waiting for transfers between devices: 181 us -> 152 us
  Pallas kernels: 74.7 us -> 84.4 us
  starting transfers between devices: 50.9 us -> 57.2 us
    all_to_all x1 -> x2, waiting for transfers between devices: 125 us -> 91.1 us  [exchange(): lax.all_to_all(blocks, ('seq', 'exp'), split_axis=0, concat_axis=0, tiled...]
    pallas_call x2 -> x4, Pallas kernels: 50.5 us -> 60.3 us  [the longest x2 43.1 us: run_expert(): pl.pallas_call(main_kernel if main else extra_kernel, grid=(2 * QUARTERS,...]
    all_to_all x1 -> x2, starting transfers between devices: 7.34 us -> 17.1 us  [exchange(): lax.all_to_all(blocks, ('seq', 'exp'), split_axis=0, concat_axis=0, tiled...]
  transfers between devices with their start and end apart: 22 -> 23, of which waited for: 13 -> 15; matrix products, arithmetic and copies ran while one was open for 5% -> 5% of each run, Pallas kernels for 0% -> 8%
where the time goes in v3:
time: 454 us; the launch traced here: 453 us
  waiting for transfers between devices  152 us (33%)
  blocking collectives  126 us (28%)
  Pallas kernels  84.4 us (19%)
  starting transfers between devices  57.2 us (13%)
  matrix products  11.9 us (3%)
  other arithmetic  10.5 us (2%)
  local copies, waits for them, and re-layouts  9.94 us (2%)
    all_to_all x1, blocking collectives, exchange(): lax.all_to_all(blocks, ('seq', 'exp'), split_axis=0, concat_axis=0, tiled...  126 us
    all_to_all x2, waiting for transfers between devices, exchange(): lax.all_to_all(blocks, ('seq', 'exp'), split_axis=0, concat_axis=0, tiled...  91.1 us
    pallas_call x2, Pallas kernels, run_expert(): pl.pallas_call(main_kernel if main else extra_kernel, grid=(2 * QUARTERS,...  43.1 us
    ppermute x7, waiting for transfers between devices, layer(): sums[index] = lax.ppermute(sums[index], ('seq', 'exp'), around)  31.5 us
    ppermute x6, waiting for transfers between devices, gather_plane(): gathered.append(lax.ppermute(line, 'exp', shifts(d)))  23.9 us
    pallas_call x2, Pallas kernels, combine(): pl.pallas_call(combine_main if main else combine_extra, grid=(QUARTERS,),...  17.2 us
    all_to_all x2, starting transfers between devices, exchange(): lax.all_to_all(blocks, ('seq', 'exp'), split_axis=0, concat_axis=0, tiled...  17.1 us
    ppermute x7, starting transfers between devices, layer(): sums[index] = lax.ppermute(sums[index], ('seq', 'exp'), around)  15.5 us
  transfers between devices with their start and end apart: 23, of which 15 were waited for; matrix products, arithmetic and copies ran while one was open for 5% of the time, Pallas kernels for 8%

profile of v3, /device:TPU:10, one launch (start us, length us, event | category | flops | bytes accessed | tf_op | source)
XLA Modules:
  0.0 453.0 jit_solution(17693781255007059419)
XLA Ops:
  6.0 4.9 %all-to-all-start = ((bf16[4,128,1280]{2,1,0:T(8,128)(2,1)}), bf16[4,128,1280]{2,1,0:T(8,128)(2,1)S(1)}, u32[]{:S(2)}, u32[]{:S(2)}) async-start(bf16[4,128,1280]{2,1,0:T(8,128)(2,1)} %maximum_bitcast_fusion), calls=%async_computation | async-start | bytes 2621440 | tf_op jit(solution)/shard_map/all_to_all | solution.py:438
  15.8 4.0 collective-permute-start.5
  29.2 3.6 collective-permute-start.8
  34.3 7.6 %fusion.20 = (f32[8,512]{1,0:T(8,128)S(1)}, f32[8,512,512]{1,2,0:T(8,128)}) fusion(pred[512,512]{0,1:T(8,128)(4,1)} %fusion.9, bf16[512,8,128]{0,2,1:T(8,128)(2,1)} %bitcast.103, bf16[512,1280]{1,0:T(8,128)(2,1)S(1)} %bitcast.94), kind=kOutput, calls=%fused_computation.56 | convolution fusion | flops 545260032 | bytes 9846784 | tf_op jit(solution)/shard_map/sub | solution.py:37
  41.8 4.2 fusion.6
  50.3 4.3 collective-permute-done.8.rest_2_
  56.1 4.9 %collective-permute-done.9.rest_3_ = bf16[4,512,128]{2,1,0:T(8,128)(2,1)} collective-permute-done((bf16[4,512,128]{2,1,0:T(8,128)(2,1)S(1)}, bf16[4,512,128]{2,1,0:T(8,128)(2,1)}, u32[]{:S(2)}, u32[]{:S(2)}) %collective-permute-start.9) | collective-permute-done | bytes 524320 | tf_op jit(solution)/shard_map/ppermute | solution.py:62
  62.6 3.0 collective-permute-done.11.rest_6_
  65.7 10.1 %collective-permute-done.12.rest_7_ = bf16[4,512,128]{2,1,0:T(8,128)(2,1)} collective-permute-done((bf16[4,512,128]{2,1,0:T(8,128)(2,1)S(1)}, bf16[4,512,128]{2,1,0:T(8,128)(2,1)}, u32[]{:S(2)}, u32[]{:S(2)}) %collective-permute-start.12) | collective-permute-done | bytes 524320 | tf_op jit(solution)/shard_map/ppermute | solution.py:62
  76.7 11.5 %project.1 = (f32[128,2048]{1,0:T(8,128)}, bf16[128,2048]{1,0:T(8,128)(2,1)}, bf16[128,2048]{1,0:T(8,128)(2,1)}, bf16[128,2048]{1,0:T(8,128)(2,1)}, bf16[128,204...) custom-call(s32[4]{0:T(128)} %pad_add_fusion.place, ...), custom_call_target="tpu_custom_call" | custom-call | tf_op jit(solution)/shard_map/project/pallas_call | solution.py:111
  88.5 3.5 collective-permute-start.14
  94.6 8.9 %collective-permute-done.13.refs_1_ = bf16[128,2048]{1,0:T(8,128)(2,1)S(1)} collective-permute-done((bf16[128,2048]{1,0:T(8,128)(2,1)}, bf16[128,2048]{1,0:T(8,128)(2,1)S(1)}, u32[]{:S(2)}, u32[]{:S(2)}) %collective-permute-start.13) | collective-permute-done | bytes 524320 | tf_op jit(solution)/shard_map/ppermute | solution.py:460
  105.1 9.5 %collective-permute-start.19 = (bf16[128,2048]{1,0:T(8,128)(2,1)}, bf16[128,2048]{1,0:T(8,128)(2,1)}, u32[]{:S(2)}, u32[]{:S(2)}) collective-permute-start(bf16[128,2048]{1,0:T(8,128)(2,1)} %get-tuple-element.29), channel_id=1, source_target_pairs={{0,97},{1,96},{2,99},{3,98},{4,101},{5,100},{6,103},{7,102},{8,105... | collective-permute-start | bytes 1572872 | tf_op jit(solution)/shard_map/ppermute | solution.py:460
  116.9 7.2 %collective-permute-done.17.refs_5_ = bf16[128,2048]{1,0:T(8,128)(2,1)S(1)} collective-permute-done((bf16[128,2048]{1,0:T(8,128)(2,1)}, bf16[128,2048]{1,0:T(8,128)(2,1)S(1)}, u32[]{:S(2)}, u32[]{:S(2)}) %collective-permute-start.17) | collective-permute-done | bytes 524320 | tf_op jit(solution)/shard_map/ppermute | solution.py:460
  124.7 13.3 %collective-permute-done.19.refs_7_ = bf16[128,2048]{1,0:T(8,128)(2,1)} collective-permute-done((bf16[128,2048]{1,0:T(8,128)(2,1)}, bf16[128,2048]{1,0:T(8,128)(2,1)}, u32[]{:S(2)}, u32[]{:S(2)}) %collective-permute-start.19) | collective-permute-done | bytes 524320 | tf_op jit(solution)/shard_map/ppermute | solution.py:460
  138.0 12.7 %norm_pack.1 = (f32[128,4096]{1,0:T(8,128)}, bf16[1024,5120]{1,0:T(8,128)(2,1)}) custom-call(s32[4]{0:T(128)} %pad_add_fusion.place, f32[128,2048]{1,0:T(8,128)} %get-tuple-element.22.refs_0_, bf16[128,2048]{1,0:T(8,128)(2,1)} %copy-done.5, bf16[128,2048]{1,0:T(8,128)(2,1)} %copy-done.6, bf16[128,2048]{1,0:T(8,128)(2,1)} %copy-done.7, ...), custom_call_target="tpu_custom_call" | custom-call | tf_op jit(solution)/shard_map/norm_pack/pallas_call | solution.py:173
  150.7 126.1 %all_to_all.20 = bf16[128,8,5120]{2,1,0:T(8,128)(2,1)} all-to-all(bf16[128,8,5120]{2,1,0:T(8,128)(2,1)} %bitcast.91), channel_id=1, replica_groups=mesh['seq'=4,'exp'=32] {'seq','exp'}, dimensions={0} | all-to-all | bytes 20971520 | tf_op jit(solution)/shard_map/all_to_all | solution.py:467
  276.8 15.4 %experts_extra.1.after = bf16[1024,1024]{1,0:T(8,128)(2,1)} custom-call(bf16[1024,5120]{1,0:T(8,128)(2,1)} %bitcast.83, bf16[4096,1536]{1,0:T(8,128)(2,1)} %bitcast.85, bf16[768,4096]{1,0:T(8,128)(2,1)} %bitcast.88), custom_call_target="tpu_custom_call" | custom-call | tf_op jit(solution)/shard_map/experts_extra/pallas_call | solution.py:287
  292.1 6.9 %all-to-all-start.3 = ((bf16[128,8,1024]{2,1,0:T(8,128)(2,1)}), bf16[128,8,1024]{2,1,0:T(8,128)(2,1)S(1)}, u32[]{:S(2)}, u32[]{:S(2)}) async-start(bf16[128,8,1024]{2,1,0:T(8,128)(2,1)} %bitcast.90), calls=%async_computation.3 | async-start | bytes 4194304 | tf_op jit(solution)/shard_map/all_to_all | solution.py:467
  299.1 27.7 %experts_main.1 = bf16[1024,4096]{1,0:T(8,128)(2,1)} custom-call(bf16[1024,1024]{1,0:T(8,128)(2,1)} %experts_extra.1.after, bf16[1024,5120]{1,0:T(8,128)(2,1)} %bitcast.84, bf16[4096,1536]{1,0:T(8,128)(2,1)} %bitcast.86, bf16[768,4096]{1,0:T(8,128)(2,1)} %bitcast.89), custom_call_target="tpu_custom_call" | custom-call | tf_op jit(solution)/shard_map/experts_main/pallas_call | solution.py:287
  328.2 10.1 %all-to-all-start.2 = ((bf16[128,8,4096]{2,1,0:T(8,128)(2,1)}), bf16[128,8,4096]{2,1,0:T(8,128)(2,1)}, u32[]{:S(2)}, u32[]{:S(2)}) async-start(bf16[128,8,4096]{2,1,0:T(8,128)(2,1)} %bitcast.87), calls=%async_computation.2 | async-start | bytes 16777216 | tf_op jit(solution)/shard_map/all_to_all | solution.py:467
  344.8 7.1 %combine_extra.1 = (f32[128,4096]{1,0:T(8,128)}, f32[128,128]{1,0:T(8,128)}) custom-call(bf16[1024,1024]{1,0:T(8,128)(2,1)} %bitcast.92, f32[128,4096]{1,0:T(8,128)} %get-tuple-element.31.hidden, bf16[128,4096]{1,0:T(8,128)(2,1)} %bitcast.96, bf16[256,256]{1,0:T(8,128)(2,1)} %pad_maximum_fusion.3.gates, s32[128,8]{1,0:T(8,128)} %get-tuple-element.41.keys), custom_call_target="tpu_custom_call" | custom-call | tf_op jit(solution)/shard_map/combine_extra/pallas_call | solution.py:362
  351.9 91.0 %all-to-all-done.2 = bf16[128,8,4096]{2,1,0:T(8,128)(2,1)} async-done(((bf16[128,8,4096]{2,1,0:T(8,128)(2,1)}), bf16[128,8,4096]{2,1,0:T(8,128)(2,1)}, u32[]{:S(2)}, u32[]{:S(2)}) %all-to-all-start.2) | async-done | bytes 8388640 | tf_op jit(solution)/shard_map/all_to_all | solution.py:467
  442.9 10.1 %combine_main.1 = (bf16[128,4096]{1,0:T(8,128)(2,1)}, f32[8,128]{1,0:T(8,128)}) custom-call(bf16[1024,4096]{1,0:T(8,128)(2,1)} %bitcast.33.main, f32[128,4096]{1,0:T(8,128)} %get-tuple-element.32.hidden, bf16[128,4096]{1,0:T(8,128)(2,1)} %bitcast.97, bf16[256,1024]{1,0:T(8,128)(2,1)} %pad_maximum_fusion.2.gates, s32[128,8]{1,0:T(8,128)} %get-tuple-element.40.keys, ...), custom_call_target="tpu_custom_call" | custom-call | tf_op jit(solution)/shard_map/combine_main/pallas_call | solution.py:362
  (111 shorter events, 44.3 us)
Async XLA Ops:
  6.0 21.5 %all-to-all-start = ((bf16[4,128,1280]{2,1,0:T(8,128)(2,1)}), bf16[4,128,1280]{2,1,0:T(8,128)(2,1)S(1)}, u32[]{:S(2)}, u32[]{:S(2)}) async-start(bf16[4,128,1280]{2,1,0:T(8,128)(2,1)} %maximum_bitcast_fusion), calls=%async_computation | async-start | bytes 2621440 | tf_op jit(solution)/shard_map/all_to_all | solution.py:438
  10.9 8.9 %collective-permute-start.2 = (bf16[512,128]{1,0:T(8,128)(2,1)S(1)}, bf16[512,128]{1,0:T(8,128)(2,1)S(1)}, u32[]{:S(2)}, u32[]{:S(2)}) collective-permute-start(bf16[512,128]{1,0:T(8,128)(2,1)S(1)} %get-tuple-element.39), channel_id=1, source_target_pairs={{0,6},{1,7},{2,0},{3,1},{4,2},{5,3},{6,4},{7,5},{8,14},{9,15},{10,... | collective-permute-start | bytes 393224 | tf_op jit(solution)/shard_map/ppermute | solution.py:56
  11.5 10.5 %collective-permute-start.1 = (bf16[512,128]{1,0:T(8,128)(2,1)S(1)}, bf16[512,128]{1,0:T(8,128)(2,1)S(1)}, u32[]{:S(2)}, u32[]{:S(2)}) collective-permute-start(bf16[512,128]{1,0:T(8,128)(2,1)S(1)} %get-tuple-element.39), channel_id=1, source_target_pairs={{0,4},{1,5},{2,6},{3,7},{4,0},{5,1},{6,2},{7,3},{8,12},{9,13},{10,... | collective-permute-start | bytes 393224 | tf_op jit(solution)/shard_map/ppermute | solution.py:56
  14.0 8.0 %collective-permute-start = (bf16[512,128]{1,0:T(8,128)(2,1)S(1)}, bf16[512,128]{1,0:T(8,128)(2,1)S(1)}, u32[]{:S(2)}, u32[]{:S(2)}) collective-permute-start(bf16[512,128]{1,0:T(8,128)(2,1)S(1)} %get-tuple-element.39), channel_id=1, source_target_pairs={{0,2},{1,3},{2,4},{3,5},{4,6},{5,7},{6,0},{7,1},{8,10},{9,11},{10,... | collective-permute-start | bytes 393224 | tf_op jit(solution)/shard_map/ppermute | solution.py:56
  15.8 8.2 %collective-permute-start.5 = (bf16[512,128]{1,0:T(8,128)(2,1)S(1)}, bf16[512,128]{1,0:T(8,128)(2,1)S(1)}, u32[]{:S(2)}, u32[]{:S(2)}) collective-permute-start(bf16[512,128]{1,0:T(8,128)(2,1)S(1)} %get-tuple-element.38), channel_id=1, source_target_pairs={{0,24},{1,25},{2,26},{3,27},{4,28},{5,29},{6,30},{7,31},{8,0},{9,1... | collective-permute-start | bytes 393224 | tf_op jit(solution)/shard_map/ppermute | solution.py:56
  19.8 6.6 %collective-permute-start.4 = (bf16[512,128]{1,0:T(8,128)(2,1)S(1)}, bf16[512,128]{1,0:T(8,128)(2,1)S(1)}, u32[]{:S(2)}, u32[]{:S(2)}) collective-permute-start(bf16[512,128]{1,0:T(8,128)(2,1)S(1)} %get-tuple-element.38), channel_id=1, source_target_pairs={{0,16},{1,17},{2,18},{3,19},{4,20},{5,21},{6,22},{7,23},{8,24},{9,... | collective-permute-start | bytes 393224 | tf_op jit(solution)/shard_map/ppermute | solution.py:56
  19.8 7.6 %collective-permute-start.3 = (bf16[512,128]{1,0:T(8,128)(2,1)S(1)}, bf16[512,128]{1,0:T(8,128)(2,1)S(1)}, u32[]{:S(2)}, u32[]{:S(2)}) collective-permute-start(bf16[512,128]{1,0:T(8,128)(2,1)S(1)} %get-tuple-element.38), channel_id=1, source_target_pairs={{0,8},{1,9},{2,10},{3,11},{4,12},{5,13},{6,14},{7,15},{8,16},{9,17... | collective-permute-start | bytes 393224 | tf_op jit(solution)/shard_map/ppermute | solution.py:56
  27.5 21.7 %collective-permute-start.7 = (bf16[4,512,128]{2,1,0:T(8,128)(2,1)S(1)}, bf16[4,512,128]{2,1,0:T(8,128)(2,1)}, u32[]{:S(2)}, u32[]{:S(2)}) collective-permute-start(bf16[4,512,128]{2,1,0:T(8,128)(2,1)S(1)} %pad_maximum_fusion.rest_0_), channel_id=1, source_target_pairs={{0,8},{1,9},{2,10},{3,11},{4,12},{5,13},{6,14},{7,15},{8,16},{9,17... | collective-permute-start | bytes 1572872 | tf_op jit(solution)/shard_map/ppermute | solution.py:62
  29.2 25.4 %collective-permute-start.8 = (bf16[4,512,128]{2,1,0:T(8,128)(2,1)S(1)}, bf16[4,512,128]{2,1,0:T(8,128)(2,1)}, u32[]{:S(2)}, u32[]{:S(2)}) collective-permute-start(bf16[4,512,128]{2,1,0:T(8,128)(2,1)S(1)} %pad_maximum_fusion.rest_0_), channel_id=1, source_target_pairs={{0,16},{1,17},{2,18},{3,19},{4,20},{5,21},{6,22},{7,23},{8,24},{9,... | collective-permute-start | bytes 1572872 | tf_op jit(solution)/shard_map/ppermute | solution.py:62
  46.5 29.2 %collective-permute-start.6 = (bf16[512,1024]{1,0:T(8,128)(2,1)S(1)}, bf16[512,1024]{1,0:T(8,128)(2,1)S(1)}, u32[]{:S(2)}, u32[]{:S(2)}) collective-permute-start(bf16[512,1024]{1,0:T(8,128)(2,1)S(1)} %copy.63.mine), channel_id=1, source_target_pairs={{0,1},{1,0},{2,3},{3,2},{4,5},{5,4},{6,7},{7,6},{8,9},{9,8},{10,11... | collective-permute-start | bytes 3145736 | tf_op jit(solution)/shard_map/ppermute | solution.py:449
  46.7 14.4 %collective-permute-start.9 = (bf16[4,512,128]{2,1,0:T(8,128)(2,1)S(1)}, bf16[4,512,128]{2,1,0:T(8,128)(2,1)}, u32[]{:S(2)}, u32[]{:S(2)}) collective-permute-start(bf16[4,512,128]{2,1,0:T(8,128)(2,1)S(1)} %pad_maximum_fusion.rest_0_), channel_id=1, source_target_pairs={{0,24},{1,25},{2,26},{3,27},{4,28},{5,29},{6,30},{7,31},{8,0},{9,1... | collective-permute-start | bytes 1572872 | tf_op jit(solution)/shard_map/ppermute | solution.py:62
  47.7 14.9 %collective-permute-start.10 = (bf16[4,512,128]{2,1,0:T(8,128)(2,1)S(1)}, bf16[4,512,128]{2,1,0:T(8,128)(2,1)}, u32[]{:S(2)}, u32[]{:S(2)}) collective-permute-start(bf16[4,512,128]{2,1,0:T(8,128)(2,1)S(1)} %pad_maximum_fusion.1.rest_4_), channel_id=1, source_target_pairs={{0,2},{1,3},{2,4},{3,5},{4,6},{5,7},{6,0},{7,1},{8,10},{9,11},{10,... | collective-permute-start | bytes 1572872 | tf_op jit(solution)/shard_map/ppermute | solution.py:62
  49.2 16.5 %collective-permute-start.11 = (bf16[4,512,128]{2,1,0:T(8,128)(2,1)S(1)}, bf16[4,512,128]{2,1,0:T(8,128)(2,1)}, u32[]{:S(2)}, u32[]{:S(2)}) collective-permute-start(bf16[4,512,128]{2,1,0:T(8,128)(2,1)S(1)} %pad_maximum_fusion.1.rest_4_), channel_id=1, source_target_pairs={{0,4},{1,5},{2,6},{3,7},{4,0},{5,1},{6,2},{7,3},{8,12},{9,13},{10,... | collective-permute-start | bytes 1572872 | tf_op jit(solution)/shard_map/ppermute | solution.py:62
  54.7 21.1 %collective-permute-start.12 = (bf16[4,512,128]{2,1,0:T(8,128)(2,1)S(1)}, bf16[4,512,128]{2,1,0:T(8,128)(2,1)}, u32[]{:S(2)}, u32[]{:S(2)}) collective-permute-start(bf16[4,512,128]{2,1,0:T(8,128)(2,1)S(1)} %pad_maximum_fusion.1.rest_4_), channel_id=1, source_target_pairs={{0,6},{1,7},{2,0},{3,1},{4,2},{5,3},{6,4},{7,5},{8,14},{9,15},{10,... | collective-permute-start | bytes 1572872 | tf_op jit(solution)/shard_map/ppermute | solution.py:62
  88.2 15.3 %collective-permute-start.13 = (bf16[128,2048]{1,0:T(8,128)(2,1)}, bf16[128,2048]{1,0:T(8,128)(2,1)S(1)}, u32[]{:S(2)}, u32[]{:S(2)}) collective-permute-start(bf16[128,2048]{1,0:T(8,128)(2,1)} %get-tuple-element.23), channel_id=1, source_target_pairs={{0,32},{1,33},{2,34},{3,35},{4,36},{5,37},{6,38},{7,39},{8,40},{9,... | collective-permute-start | bytes 1572872 | tf_op jit(solution)/shard_map/ppermute | solution.py:460
  88.5 16.6 %collective-permute-start.14 = (bf16[128,2048]{1,0:T(8,128)(2,1)}, bf16[128,2048]{1,0:T(8,128)(2,1)S(1)}, u32[]{:S(2)}, u32[]{:S(2)}) collective-permute-start(bf16[128,2048]{1,0:T(8,128)(2,1)} %get-tuple-element.24), channel_id=1, source_target_pairs={{0,64},{1,65},{2,66},{3,67},{4,68},{5,69},{6,70},{7,71},{8,72},{9,... | collective-permute-start | bytes 1572872 | tf_op jit(solution)/shard_map/ppermute | solution.py:460
  92.4 24.5 %collective-permute-start.15 = (bf16[128,2048]{1,0:T(8,128)(2,1)}, bf16[128,2048]{1,0:T(8,128)(2,1)S(1)}, u32[]{:S(2)}, u32[]{:S(2)}) collective-permute-start(bf16[128,2048]{1,0:T(8,128)(2,1)} %get-tuple-element.25), channel_id=1, source_target_pairs={{0,96},{1,97},{2,98},{3,99},{4,100},{5,101},{6,102},{7,103},{8,104... | collective-permute-start | bytes 1572872 | tf_op jit(solution)/shard_map/ppermute | solution.py:460
  93.1 23.9 %collective-permute-start.16 = (bf16[128,2048]{1,0:T(8,128)(2,1)}, bf16[128,2048]{1,0:T(8,128)(2,1)S(1)}, u32[]{:S(2)}, u32[]{:S(2)}) collective-permute-start(bf16[128,2048]{1,0:T(8,128)(2,1)} %get-tuple-element.26), channel_id=1, source_target_pairs={{0,1},{1,0},{2,3},{3,2},{4,5},{5,4},{6,7},{7,6},{8,9},{9,8},{10,11... | collective-permute-start | bytes 1572872 | tf_op jit(solution)/shard_map/ppermute | solution.py:460
  93.1 31.0 %collective-permute-start.17 = (bf16[128,2048]{1,0:T(8,128)(2,1)}, bf16[128,2048]{1,0:T(8,128)(2,1)S(1)}, u32[]{:S(2)}, u32[]{:S(2)}) collective-permute-start(bf16[128,2048]{1,0:T(8,128)(2,1)} %get-tuple-element.27), channel_id=1, source_target_pairs={{0,33},{1,32},{2,35},{3,34},{4,37},{5,36},{6,39},{7,38},{8,41},{9,... | collective-permute-start | bytes 1572872 | tf_op jit(solution)/shard_map/ppermute | solution.py:460
  103.5 34.5 %copy-start.5 = (bf16[128,2048]{1,0:T(8,128)(2,1)}, bf16[128,2048]{1,0:T(8,128)(2,1)S(1)}, u32[]{:S(2)}) copy-start(bf16[128,2048]{1,0:T(8,128)(2,1)S(1)} %collective-permute-done.13.refs_1_) | copy-start | bytes 1572868
  103.5 21.2 %collective-permute-start.18 = (bf16[128,2048]{1,0:T(8,128)(2,1)}, bf16[128,2048]{1,0:T(8,128)(2,1)S(1)}, u32[]{:S(2)}, u32[]{:S(2)}) collective-permute-start(bf16[128,2048]{1,0:T(8,128)(2,1)} %get-tuple-element.28), channel_id=1, source_target_pairs={{0,65},{1,64},{2,67},{3,66},{4,69},{5,68},{6,71},{7,70},{8,73},{9,... | collective-permute-start | bytes 1572872 | tf_op jit(solution)/shard_map/ppermute | solution.py:460
  105.1 32.9 %collective-permute-start.19 = (bf16[128,2048]{1,0:T(8,128)(2,1)}, bf16[128,2048]{1,0:T(8,128)(2,1)}, u32[]{:S(2)}, u32[]{:S(2)}) collective-permute-start(bf16[128,2048]{1,0:T(8,128)(2,1)} %get-tuple-element.29), channel_id=1, source_target_pairs={{0,97},{1,96},{2,99},{3,98},{4,101},{5,100},{6,103},{7,102},{8,105... | collective-permute-start | bytes 1572872 | tf_op jit(solution)/shard_map/ppermute | solution.py:460
  292.1 34.8 %all-to-all-start.3 = ((bf16[128,8,1024]{2,1,0:T(8,128)(2,1)}), bf16[128,8,1024]{2,1,0:T(8,128)(2,1)S(1)}, u32[]{:S(2)}, u32[]{:S(2)}) async-start(bf16[128,8,1024]{2,1,0:T(8,128)(2,1)} %bitcast.90), calls=%async_computation.3 | async-start | bytes 4194304 | tf_op jit(solution)/shard_map/all_to_all | solution.py:467
  328.2 114.7 %all-to-all-start.2 = ((bf16[128,8,4096]{2,1,0:T(8,128)(2,1)}), bf16[128,8,4096]{2,1,0:T(8,128)(2,1)}, u32[]{:S(2)}, u32[]{:S(2)}) async-start(bf16[128,8,4096]{2,1,0:T(8,128)(2,1)} %bitcast.87), calls=%async_computation.2 | async-start | bytes 16777216 | tf_op jit(solution)/shard_map/all_to_all | solution.py:467
  (14 other events, 233.5 us)

commit v4 on v3

--- a/solution.py
+++ b/solution.py
@@ -183,7 +183,7 @@
             jax.ShapeDtypeStruct((tokens, width), F32),
             jax.ShapeDtypeStruct((slots, width + quarter), BF),
         ],
-        compiler_params=pltpu.CompilerParams(vmem_limit_bytes=VMEM_LIMIT),
+        compiler_params=pltpu.CompilerParams(vmem_limit_bytes=24 * 1024 * 1024),
         name="norm_pack",
     )(place, *sums, residual, gain, main_hot, extra_hot)
 
@@ -216,7 +216,7 @@
         out[g * size : (g + 1) * size, :] = dot(swap, rows).astype(BF)
 
 
-def up_step(step, rows, w_in, acc, act):
+def up_step(step, rows, weights, acc, act):
     hidden = act.shape[1]
 
     @pl.when(step == 0)
@@ -225,7 +225,7 @@
         def _(r):
             acc[pl.ds(pl.multiple_of(r * 64, 64), 64), :] = jnp.zeros((64, acc.shape[1]), F32)
 
-    acc[...] += dot(rows, w_in[...])
+    acc[...] += dot(rows, weights)
 
     @pl.when(step == QUARTERS - 1)
     def _():
@@ -238,7 +238,7 @@
 
     @pl.when(step < QUARTERS)
     def _():
-        up_step(step, main[...], w_in, acc, act)
+        up_step(step, main[...], w_in[...], acc, act)
 
     @pl.when(step >= QUARTERS)
     def _():
@@ -254,11 +254,14 @@
 
     @pl.when(step < QUARTERS)
     def _():
-        up_step(step, parts[step], w_in, acc, act)
+        rows = w_in.shape[0] // QUARTERS
+        up_step(step, parts[step], w_in[pl.ds(pl.multiple_of(step * rows, rows), rows), :], acc, act)
 
     @pl.when(step >= QUARTERS)
     def _():
-        parts[step - QUARTERS] = dot(act[...], w_down[...]).astype(BF)
+        columns = w_down.shape[1] // QUARTERS
+        lanes = pl.ds(pl.multiple_of((step - QUARTERS) * columns, columns), columns)
+        parts[step - QUARTERS] = dot(act[...], w_down[:, lanes]).astype(BF)
 
     @pl.when(step == 2 * QUARTERS - 1)
     def _():
@@ -288,14 +291,18 @@
         main_kernel if main else extra_kernel,
         grid=(2 * QUARTERS,),
         in_specs=in_specs
-        + [
-            pl.BlockSpec((quarter, 2 * hidden), lambda i: (jnp.minimum(i, last), 0)),
-            pl.BlockSpec((hidden, quarter), lambda i: (0, jnp.clip(i - QUARTERS, 0, last))),
-        ],
+        + (
+            [
+                pl.BlockSpec((quarter, 2 * hidden), lambda i: (jnp.minimum(i, last), 0)),
+                pl.BlockSpec((hidden, quarter), lambda i: (0, jnp.clip(i - QUARTERS, 0, last))),
+            ]
+            if main
+            else [pl.BlockSpec(memory_space=pltpu.VMEM)] * 2
+        ),
         out_specs=out_specs,
         out_shape=jax.ShapeDtypeStruct((slots, out_width), BF),
         scratch_shapes=[pltpu.VMEM((rows, 2 * hidden), F32), pltpu.VMEM((rows, hidden), BF)] + scratch,
-        compiler_params=pltpu.CompilerParams(vmem_limit_bytes=VMEM_LIMIT),
+        compiler_params=pltpu.CompilerParams(vmem_limit_bytes=VMEM_LIMIT if main else 20 * 1024 * 1024),
         name="experts_main" if main else "experts_extra",
     )(*([after] if main else []), incoming, w_in, w_down)
 
@@ -375,7 +382,7 @@
         ],
         scratch_shapes=[pltpu.VMEM((tokens, count), F32)]
         + ([] if main else [pltpu.VMEM((QUARTERS, count, quarter), BF)]),
-        compiler_params=pltpu.CompilerParams(vmem_limit_bytes=VMEM_LIMIT),
+        compiler_params=pltpu.CompilerParams(vmem_limit_bytes=VMEM_LIMIT if main else 20 * 1024 * 1024),
         name="combine_main" if main else "combine_extra",
     )(returned, hidden, cot, gates, keys, *more)
 

time: 454 us -> 448 us (0.987)
  local copies, waits for them, and re-layouts: 9.94 us -> 23.5 us
  Pallas kernels: 84.4 us -> 72.9 us
  waiting for transfers between devices: 152 us -> 143 us
    all_to_all x2, waiting for transfers between devices: 91.1 us -> 81.7 us  [exchange(): lax.all_to_all(blocks, ('seq', 'exp'), split_axis=0, concat_axis=0, tiled...]
    eq x4, local copies, waits for them, and re-layouts: 0.33 us -> 5.27 us  [routing(): is_main = rank[:, :, None] == jnp.arange(MAIN, dtype=jnp.int32)]
  transfers between devices with their start and end apart: 23 -> 23, of which waited for: 15 -> 14; matrix products, arithmetic and copies ran while one was open for 5% -> 8% of each run, Pallas kernels for 8% -> 7%
where the time goes in v4:
time: 448 us; the launch traced here: 447 us
  waiting for transfers between devices  143 us (32%)
  blocking collectives  126 us (28%)
  Pallas kernels  72.9 us (16%)
  starting transfers between devices  57.3 us (13%)
  local copies, waits for them, and re-layouts  23.5 us (5%)
  matrix products  12.8 us (3%)
  other arithmetic  10.7 us (2%)
    all_to_all x1, blocking collectives, exchange(): lax.all_to_all(blocks, ('seq', 'exp'), split_axis=0, concat_axis=0, tiled...  126 us
    all_to_all x2, waiting for transfers between devices, exchange(): lax.all_to_all(blocks, ('seq', 'exp'), split_axis=0, concat_axis=0, tiled...  81.7 us
    pallas_call x2, Pallas kernels, run_expert(): pl.pallas_call(main_kernel if main else extra_kernel, grid=(2 * QUARTERS,...  39 us
    ppermute x7, waiting for transfers between devices, layer(): sums[index] = lax.ppermute(sums[index], ('seq', 'exp'), around)  31.8 us
    ppermute x6, waiting for transfers between devices, gather_plane(): gathered.append(lax.ppermute(line, 'exp', shifts(d)))  23.8 us
    all_to_all x2, starting transfers between devices, exchange(): lax.all_to_all(blocks, ('seq', 'exp'), split_axis=0, concat_axis=0, tiled...  17.1 us
    ppermute x7, starting transfers between devices, layer(): sums[index] = lax.ppermute(sums[index], ('seq', 'exp'), around)  15.4 us
    pallas_call x2, Pallas kernels, combine(): pl.pallas_call(combine_main if main else combine_extra, grid=(QUARTERS,),...  13.9 us
  transfers between devices with their start and end apart: 23, of which 14 were waited for; matrix products, arithmetic and copies ran while one was open for 8% of the time, Pallas kernels for 7%

profile of v4, /device:TPU:10, one launch (start us, length us, event | category | flops | bytes accessed | tf_op | source)
XLA Modules:
  0.0 446.7 jit_solution(5391396444518047826)
XLA Ops:
  6.0 4.9 %all-to-all-start = ((bf16[4,128,1280]{2,1,0:T(8,128)(2,1)}), bf16[4,128,1280]{2,1,0:T(8,128)(2,1)S(1)}, u32[]{:S(2)}, u32[]{:S(2)}) async-start(bf16[4,128,1280]{2,1,0:T(8,128)(2,1)} %maximum_bitcast_fusion), calls=%async_computation | async-start | bytes 2621440 | tf_op jit(solution)/shard_map/all_to_all | solution.py:445
  11.6 2.4 collective-permute-start.1
  15.8 4.0 collective-permute-start.5
  29.3 3.6 collective-permute-start.8
  34.3 7.6 %fusion.20 = (f32[8,512]{1,0:T(8,128)S(1)}, f32[8,512,512]{1,2,0:T(8,128)}) fusion(pred[512,512]{0,1:T(8,128)(4,1)} %fusion.9, bf16[512,8,128]{0,2,1:T(8,128)(2,1)} %bitcast.107, bf16[512,1280]{1,0:T(8,128)(2,1)S(1)} %bitcast.101), kind=kOutput, calls=%fused_computation.56 | convolution fusion | flops 545260032 | bytes 9846784 | tf_op jit(solution)/shard_map/sub | solution.py:37
  41.9 5.1 %fusion.6 = bf16[128,8,512]{2,0,1:T(8,128)(2,1)} fusion(f32[8,512,512]{1,2,0:T(8,128)} %get-tuple-element.43, f32[8,512]{1,0:T(8,128)S(1)} %get-tuple-element.42, bf16[512,1280]{1,0:T(8,128)(2,1)S(1)} %bitcast.102), kind=kOutput, calls=%fused_computation.10 | convolution fusion | flops 541589504 | bytes 9584640 | tf_op jit(solution)/shard_map/grj,jd->rgd/dot_general | solution.py:39
  56.2 6.8 %collective-permute-done.9.rest_3_ = bf16[4,512,128]{2,1,0:T(8,128)(2,1)} collective-permute-done((bf16[4,512,128]{2,1,0:T(8,128)(2,1)S(1)}, bf16[4,512,128]{2,1,0:T(8,128)(2,1)}, u32[]{:S(2)}, u32[]{:S(2)}) %collective-permute-start.9) | collective-permute-done | bytes 524320 | tf_op jit(solution)/shard_map/ppermute | solution.py:62
  64.6 3.0 collective-permute-done.11.rest_6_
  67.6 10.1 %collective-permute-done.12.rest_7_ = bf16[4,512,128]{2,1,0:T(8,128)(2,1)} collective-permute-done((bf16[4,512,128]{2,1,0:T(8,128)(2,1)S(1)}, bf16[4,512,128]{2,1,0:T(8,128)(2,1)}, u32[]{:S(2)}, u32[]{:S(2)}) %collective-permute-start.12) | collective-permute-done | bytes 524320 | tf_op jit(solution)/shard_map/ppermute | solution.py:62
  77.7 11.5 %project.1 = (f32[128,2048]{1,0:T(8,128)}, bf16[128,2048]{1,0:T(8,128)(2,1)}, bf16[128,2048]{1,0:T(8,128)(2,1)}, bf16[128,2048]{1,0:T(8,128)(2,1)}, bf16[128,204...) custom-call(s32[4]{0:T(128)} %pad_add_fusion.place, ...), custom_call_target="tpu_custom_call" | custom-call | tf_op jit(solution)/shard_map/project/pallas_call | solution.py:111
  89.5 3.5 collective-permute-start.14
  95.6 8.9 %collective-permute-done.13.refs_1_ = bf16[128,2048]{1,0:T(8,128)(2,1)S(1)} collective-permute-done((bf16[128,2048]{1,0:T(8,128)(2,1)}, bf16[128,2048]{1,0:T(8,128)(2,1)S(1)}, u32[]{:S(2)}, u32[]{:S(2)}) %collective-permute-start.13) | collective-permute-done | bytes 524320 | tf_op jit(solution)/shard_map/ppermute | solution.py:467
  106.1 9.5 %collective-permute-start.19 = (bf16[128,2048]{1,0:T(8,128)(2,1)}, bf16[128,2048]{1,0:T(8,128)(2,1)}, u32[]{:S(2)}, u32[]{:S(2)}) collective-permute-start(bf16[128,2048]{1,0:T(8,128)(2,1)} %get-tuple-element.29), channel_id=1, source_target_pairs={{0,97},{1,96},{2,99},{3,98},{4,101},{5,100},{6,103},{7,102},{8,105... | collective-permute-start | bytes 1572872 | tf_op jit(solution)/shard_map/ppermute | solution.py:467
  117.7 7.5 %collective-permute-done.17.refs_5_ = bf16[128,2048]{1,0:T(8,128)(2,1)} collective-permute-done((bf16[128,2048]{1,0:T(8,128)(2,1)}, bf16[128,2048]{1,0:T(8,128)(2,1)}, u32[]{:S(2)}, u32[]{:S(2)}) %collective-permute-start.17) | collective-permute-done | bytes 524320 | tf_op jit(solution)/shard_map/ppermute | solution.py:467
  125.7 13.2 %collective-permute-done.19.refs_7_ = bf16[128,2048]{1,0:T(8,128)(2,1)} collective-permute-done((bf16[128,2048]{1,0:T(8,128)(2,1)}, bf16[128,2048]{1,0:T(8,128)(2,1)}, u32[]{:S(2)}, u32[]{:S(2)}) %collective-permute-start.19) | collective-permute-done | bytes 524320 | tf_op jit(solution)/shard_map/ppermute | solution.py:467
  140.2 8.4 %norm_pack.1 = (f32[128,4096]{1,0:T(8,128)S(1)}, bf16[1024,5120]{1,0:T(8,128)(2,1)S(1)}) custom-call(s32[4]{0:T(128)S(1)} %copy-done.9, f32[128,2048]{1,0:T(8,128)S(1)} %copy-done.6, bf16[128,2048]{1,0:T(8,128)(2,1)S(1)} %collective-permute-done.13.refs_1_, bf16[128,2048]{1,0:T(8,128)(2,1)S(1)} %collective-permute-done.14.refs_2_, ...), custom_call_target="tpu_custom_call" | custom-call | tf_op jit(solution)/shard_map/norm_pack/pallas_call | solution.py:173
  150.0 125.8 %all_to_all.20 = bf16[128,8,5120]{2,1,0:T(8,128)(2,1)S(1)} all-to-all(bf16[128,8,5120]{2,1,0:T(8,128)(2,1)S(1)} %bitcast.93), channel_id=1, replica_groups=mesh['seq'=4,'exp'=32] {'seq','exp'}, dimensions={0} | all-to-all | bytes 20971520 | tf_op jit(solution)/shard_map/all_to_all | solution.py:474
  275.9 10.5 %experts_extra.1.after = bf16[1024,1024]{1,0:T(8,128)(2,1)} custom-call(bf16[1024,5120]{1,0:T(8,128)(2,1)S(1)} %bitcast.83, bf16[4096,1536]{1,0:T(8,128)(2,1)S(1)} %bitcast.88, bf16[768,4096]{1,0:T(8,128)(2,1)S(1)} %bitcast.92), custom_call_target="tpu_custom_call" | custom-call | tf_op jit(solution)/shard_map/experts_extra/pallas_call | solution.py:290
  286.4 6.9 %all-to-all-start.3 = ((bf16[128,8,1024]{2,1,0:T(8,128)(2,1)}), bf16[128,8,1024]{2,1,0:T(8,128)(2,1)S(1)}, u32[]{:S(2)}, u32[]{:S(2)}) async-start(bf16[128,8,1024]{2,1,0:T(8,128)(2,1)} %bitcast.34), calls=%async_computation.3 | async-start | bytes 4194304 | tf_op jit(solution)/shard_map/all_to_all | solution.py:474
  293.3 28.6 %experts_main.1 = bf16[1024,4096]{1,0:T(8,128)(2,1)} custom-call(bf16[1024,1024]{1,0:T(8,128)(2,1)} %experts_extra.1.after, bf16[1024,5120]{1,0:T(8,128)(2,1)} %bitcast.84, bf16[4096,1536]{1,0:T(8,128)(2,1)} %bitcast.85, bf16[768,4096]{1,0:T(8,128)(2,1)} %bitcast.89), custom_call_target="tpu_custom_call" | custom-call | tf_op jit(solution)/shard_map/experts_main/pallas_call | solution.py:290
  321.9 10.2 %all-to-all-start.2 = ((bf16[128,8,4096]{2,1,0:T(8,128)(2,1)}), bf16[128,8,4096]{2,1,0:T(8,128)(2,1)}, u32[]{:S(2)}, u32[]{:S(2)}) async-start(bf16[128,8,4096]{2,1,0:T(8,128)(2,1)} %bitcast.99), calls=%async_computation.2 | async-start | bytes 16777216 | tf_op jit(solution)/shard_map/all_to_all | solution.py:474
  349.3 3.7 combine_extra.1
  354.9 81.7 %all-to-all-done.2 = bf16[128,8,4096]{2,1,0:T(8,128)(2,1)} async-done(((bf16[128,8,4096]{2,1,0:T(8,128)(2,1)}), bf16[128,8,4096]{2,1,0:T(8,128)(2,1)}, u32[]{:S(2)}, u32[]{:S(2)}) %all-to-all-start.2) | async-done | bytes 8388640 | tf_op jit(solution)/shard_map/all_to_all | solution.py:474
  436.6 10.1 %combine_main.1 = (bf16[128,4096]{1,0:T(8,128)(2,1)}, f32[8,128]{1,0:T(8,128)}) custom-call(bf16[1024,4096]{1,0:T(8,128)(2,1)} %bitcast.33.main, f32[128,4096]{1,0:T(8,128)} %copy-done.4, bf16[128,4096]{1,0:T(8,128)(2,1)} %bitcast.95, bf16[256,1024]{1,0:T(8,128)(2,1)} %pad_maximum_fusion.2.gates, s32[128,8]{1,0:T(8,128)} %get-tuple-element.40.keys, ...), custom_call_target="tpu_custom_call" | custom-call | tf_op jit(solution)/shard_map/combine_main/pallas_call | solution.py:369
  (131 shorter events, 58.0 us)
Async XLA Ops:
  6.0 21.5 %all-to-all-start = ((bf16[4,128,1280]{2,1,0:T(8,128)(2,1)}), bf16[4,128,1280]{2,1,0:T(8,128)(2,1)S(1)}, u32[]{:S(2)}, u32[]{:S(2)}) async-start(bf16[4,128,1280]{2,1,0:T(8,128)(2,1)} %maximum_bitcast_fusion), calls=%async_computation | async-start | bytes 2621440 | tf_op jit(solution)/shard_map/all_to_all | solution.py:445
  11.0 8.9 %collective-permute-start.2 = (bf16[512,128]{1,0:T(8,128)(2,1)S(1)}, bf16[512,128]{1,0:T(8,128)(2,1)S(1)}, u32[]{:S(2)}, u32[]{:S(2)}) collective-permute-start(bf16[512,128]{1,0:T(8,128)(2,1)S(1)} %get-tuple-element.39), channel_id=1, source_target_pairs={{0,6},{1,7},{2,0},{3,1},{4,2},{5,3},{6,4},{7,5},{8,14},{9,15},{10,... | collective-permute-start | bytes 393224 | tf_op jit(solution)/shard_map/ppermute | solution.py:56
  11.6 10.4 %collective-permute-start.1 = (bf16[512,128]{1,0:T(8,128)(2,1)S(1)}, bf16[512,128]{1,0:T(8,128)(2,1)S(1)}, u32[]{:S(2)}, u32[]{:S(2)}) collective-permute-start(bf16[512,128]{1,0:T(8,128)(2,1)S(1)} %get-tuple-element.39), channel_id=1, source_target_pairs={{0,4},{1,5},{2,6},{3,7},{4,0},{5,1},{6,2},{7,3},{8,12},{9,13},{10,... | collective-permute-start | bytes 393224 | tf_op jit(solution)/shard_map/ppermute | solution.py:56
  14.0 8.0 %collective-permute-start = (bf16[512,128]{1,0:T(8,128)(2,1)S(1)}, bf16[512,128]{1,0:T(8,128)(2,1)S(1)}, u32[]{:S(2)}, u32[]{:S(2)}) collective-permute-start(bf16[512,128]{1,0:T(8,128)(2,1)S(1)} %get-tuple-element.39), channel_id=1, source_target_pairs={{0,2},{1,3},{2,4},{3,5},{4,6},{5,7},{6,0},{7,1},{8,10},{9,11},{10,... | collective-permute-start | bytes 393224 | tf_op jit(solution)/shard_map/ppermute | solution.py:56
  15.8 8.2 %collective-permute-start.5 = (bf16[512,128]{1,0:T(8,128)(2,1)S(1)}, bf16[512,128]{1,0:T(8,128)(2,1)S(1)}, u32[]{:S(2)}, u32[]{:S(2)}) collective-permute-start(bf16[512,128]{1,0:T(8,128)(2,1)S(1)} %get-tuple-element.38), channel_id=1, source_target_pairs={{0,24},{1,25},{2,26},{3,27},{4,28},{5,29},{6,30},{7,31},{8,0},{9,1... | collective-permute-start | bytes 393224 | tf_op jit(solution)/shard_map/ppermute | solution.py:56
  19.8 6.6 %collective-permute-start.4 = (bf16[512,128]{1,0:T(8,128)(2,1)S(1)}, bf16[512,128]{1,0:T(8,128)(2,1)S(1)}, u32[]{:S(2)}, u32[]{:S(2)}) collective-permute-start(bf16[512,128]{1,0:T(8,128)(2,1)S(1)} %get-tuple-element.38), channel_id=1, source_target_pairs={{0,16},{1,17},{2,18},{3,19},{4,20},{5,21},{6,22},{7,23},{8,24},{9,... | collective-permute-start | bytes 393224 | tf_op jit(solution)/shard_map/ppermute | solution.py:56
  19.8 7.6 %collective-permute-start.3 = (bf16[512,128]{1,0:T(8,128)(2,1)S(1)}, bf16[512,128]{1,0:T(8,128)(2,1)S(1)}, u32[]{:S(2)}, u32[]{:S(2)}) collective-permute-start(bf16[512,128]{1,0:T(8,128)(2,1)S(1)} %get-tuple-element.38), channel_id=1, source_target_pairs={{0,8},{1,9},{2,10},{3,11},{4,12},{5,13},{6,14},{7,15},{8,16},{9,17... | collective-permute-start | bytes 393224 | tf_op jit(solution)/shard_map/ppermute | solution.py:56
  27.5 23.7 %collective-permute-start.7 = (bf16[4,512,128]{2,1,0:T(8,128)(2,1)S(1)}, bf16[4,512,128]{2,1,0:T(8,128)(2,1)}, u32[]{:S(2)}, u32[]{:S(2)}) collective-permute-start(bf16[4,512,128]{2,1,0:T(8,128)(2,1)S(1)} %pad_maximum_fusion.rest_0_), channel_id=1, source_target_pairs={{0,8},{1,9},{2,10},{3,11},{4,12},{5,13},{6,14},{7,15},{8,16},{9,17... | collective-permute-start | bytes 1572872 | tf_op jit(solution)/shard_map/ppermute | solution.py:62
  29.3 25.4 %collective-permute-start.8 = (bf16[4,512,128]{2,1,0:T(8,128)(2,1)S(1)}, bf16[4,512,128]{2,1,0:T(8,128)(2,1)}, u32[]{:S(2)}, u32[]{:S(2)}) collective-permute-start(bf16[4,512,128]{2,1,0:T(8,128)(2,1)S(1)} %pad_maximum_fusion.rest_0_), channel_id=1, source_target_pairs={{0,16},{1,17},{2,18},{3,19},{4,20},{5,21},{6,22},{7,23},{8,24},{9,... | collective-permute-start | bytes 1572872 | tf_op jit(solution)/shard_map/ppermute | solution.py:62
  48.5 29.2 %collective-permute-start.6 = (bf16[512,1024]{1,0:T(8,128)(2,1)S(1)}, bf16[512,1024]{1,0:T(8,128)(2,1)}, u32[]{:S(2)}, u32[]{:S(2)}) collective-permute-start(bf16[512,1024]{1,0:T(8,128)(2,1)S(1)} %copy.63.mine), channel_id=1, source_target_pairs={{0,1},{1,0},{2,3},{3,2},{4,5},{5,4},{6,7},{7,6},{8,9},{9,8},{10,11... | collective-permute-start | bytes 3145736 | tf_op jit(solution)/shard_map/ppermute | solution.py:456
  48.6 14.4 %collective-permute-start.9 = (bf16[4,512,128]{2,1,0:T(8,128)(2,1)S(1)}, bf16[4,512,128]{2,1,0:T(8,128)(2,1)}, u32[]{:S(2)}, u32[]{:S(2)}) collective-permute-start(bf16[4,512,128]{2,1,0:T(8,128)(2,1)S(1)} %pad_maximum_fusion.rest_0_), channel_id=1, source_target_pairs={{0,24},{1,25},{2,26},{3,27},{4,28},{5,29},{6,30},{7,31},{8,0},{9,1... | collective-permute-start | bytes 1572872 | tf_op jit(solution)/shard_map/ppermute | solution.py:62
  49.7 14.9 %collective-permute-start.10 = (bf16[4,512,128]{2,1,0:T(8,128)(2,1)S(1)}, bf16[4,512,128]{2,1,0:T(8,128)(2,1)}, u32[]{:S(2)}, u32[]{:S(2)}) collective-permute-start(bf16[4,512,128]{2,1,0:T(8,128)(2,1)S(1)} %pad_maximum_fusion.1.rest_4_), channel_id=1, source_target_pairs={{0,2},{1,3},{2,4},{3,5},{4,6},{5,7},{6,0},{7,1},{8,10},{9,11},{10,... | collective-permute-start | bytes 1572872 | tf_op jit(solution)/shard_map/ppermute | solution.py:62
  51.2 16.4 %collective-permute-start.11 = (bf16[4,512,128]{2,1,0:T(8,128)(2,1)S(1)}, bf16[4,512,128]{2,1,0:T(8,128)(2,1)}, u32[]{:S(2)}, u32[]{:S(2)}) collective-permute-start(bf16[4,512,128]{2,1,0:T(8,128)(2,1)S(1)} %pad_maximum_fusion.1.rest_4_), channel_id=1, source_target_pairs={{0,4},{1,5},{2,6},{3,7},{4,0},{5,1},{6,2},{7,3},{8,12},{9,13},{10,... | collective-permute-start | bytes 1572872 | tf_op jit(solution)/shard_map/ppermute | solution.py:62
  54.7 23.0 %collective-permute-start.12 = (bf16[4,512,128]{2,1,0:T(8,128)(2,1)S(1)}, bf16[4,512,128]{2,1,0:T(8,128)(2,1)}, u32[]{:S(2)}, u32[]{:S(2)}) collective-permute-start(bf16[4,512,128]{2,1,0:T(8,128)(2,1)S(1)} %pad_maximum_fusion.1.rest_4_), channel_id=1, source_target_pairs={{0,6},{1,7},{2,0},{3,1},{4,2},{5,3},{6,4},{7,5},{8,14},{9,15},{10,... | collective-permute-start | bytes 1572872 | tf_op jit(solution)/shard_map/ppermute | solution.py:62
  89.2 15.3 %collective-permute-start.13 = (bf16[128,2048]{1,0:T(8,128)(2,1)}, bf16[128,2048]{1,0:T(8,128)(2,1)S(1)}, u32[]{:S(2)}, u32[]{:S(2)}) collective-permute-start(bf16[128,2048]{1,0:T(8,128)(2,1)} %get-tuple-element.23), channel_id=1, source_target_pairs={{0,32},{1,33},{2,34},{3,35},{4,36},{5,37},{6,38},{7,39},{8,40},{9,... | collective-permute-start | bytes 1572872 | tf_op jit(solution)/shard_map/ppermute | solution.py:467
  89.5 16.6 %collective-permute-start.14 = (bf16[128,2048]{1,0:T(8,128)(2,1)}, bf16[128,2048]{1,0:T(8,128)(2,1)S(1)}, u32[]{:S(2)}, u32[]{:S(2)}) collective-permute-start(bf16[128,2048]{1,0:T(8,128)(2,1)} %get-tuple-element.24), channel_id=1, source_target_pairs={{0,64},{1,65},{2,66},{3,67},{4,68},{5,69},{6,70},{7,71},{8,72},{9,... | collective-permute-start | bytes 1572872 | tf_op jit(solution)/shard_map/ppermute | solution.py:467
  93.4 24.2 %collective-permute-start.15 = (bf16[128,2048]{1,0:T(8,128)(2,1)}, bf16[128,2048]{1,0:T(8,128)(2,1)S(1)}, u32[]{:S(2)}, u32[]{:S(2)}) collective-permute-start(bf16[128,2048]{1,0:T(8,128)(2,1)} %get-tuple-element.25), channel_id=1, source_target_pairs={{0,96},{1,97},{2,98},{3,99},{4,100},{5,101},{6,102},{7,103},{8,104... | collective-permute-start | bytes 1572872 | tf_op jit(solution)/shard_map/ppermute | solution.py:467
  94.1 23.6 %collective-permute-start.16 = (bf16[128,2048]{1,0:T(8,128)(2,1)}, bf16[128,2048]{1,0:T(8,128)(2,1)S(1)}, u32[]{:S(2)}, u32[]{:S(2)}) collective-permute-start(bf16[128,2048]{1,0:T(8,128)(2,1)} %get-tuple-element.26), channel_id=1, source_target_pairs={{0,1},{1,0},{2,3},{3,2},{4,5},{5,4},{6,7},{7,6},{8,9},{9,8},{10,11... | collective-permute-start | bytes 1572872 | tf_op jit(solution)/shard_map/ppermute | solution.py:467
  94.1 31.1 %collective-permute-start.17 = (bf16[128,2048]{1,0:T(8,128)(2,1)}, bf16[128,2048]{1,0:T(8,128)(2,1)}, u32[]{:S(2)}, u32[]{:S(2)}) collective-permute-start(bf16[128,2048]{1,0:T(8,128)(2,1)} %get-tuple-element.27), channel_id=1, source_target_pairs={{0,33},{1,32},{2,35},{3,34},{4,37},{5,36},{6,39},{7,38},{8,41},{9,... | collective-permute-start | bytes 1572872 | tf_op jit(solution)/shard_map/ppermute | solution.py:467
  104.5 21.2 %collective-permute-start.18 = (bf16[128,2048]{1,0:T(8,128)(2,1)}, bf16[128,2048]{1,0:T(8,128)(2,1)}, u32[]{:S(2)}, u32[]{:S(2)}) collective-permute-start(bf16[128,2048]{1,0:T(8,128)(2,1)} %get-tuple-element.28), channel_id=1, source_target_pairs={{0,65},{1,64},{2,67},{3,66},{4,69},{5,68},{6,71},{7,70},{8,73},{9,... | collective-permute-start | bytes 1572872 | tf_op jit(solution)/shard_map/ppermute | solution.py:467
  106.1 32.8 %collective-permute-start.19 = (bf16[128,2048]{1,0:T(8,128)(2,1)}, bf16[128,2048]{1,0:T(8,128)(2,1)}, u32[]{:S(2)}, u32[]{:S(2)}) collective-permute-start(bf16[128,2048]{1,0:T(8,128)(2,1)} %get-tuple-element.29), channel_id=1, source_target_pairs={{0,97},{1,96},{2,99},{3,98},{4,101},{5,100},{6,103},{7,102},{8,105... | collective-permute-start | bytes 1572872 | tf_op jit(solution)/shard_map/ppermute | solution.py:467
  140.2 135.6 %slice-start = ((s8[12582912]{0:T(1024)(128)(4,1)}), s8[4194304]{0:T(1024)(128)(4,1)S(1)}, s32[]{:S(2)}) async-start(s8[12582912]{0:T(1024)(128)(4,1)} %bitcast.86), calls=%async_computation.4 | async-start | bytes 8388608
  286.4 35.5 %all-to-all-start.3 = ((bf16[128,8,1024]{2,1,0:T(8,128)(2,1)}), bf16[128,8,1024]{2,1,0:T(8,128)(2,1)S(1)}, u32[]{:S(2)}, u32[]{:S(2)}) async-start(bf16[128,8,1024]{2,1,0:T(8,128)(2,1)} %bitcast.34), calls=%async_computation.3 | async-start | bytes 4194304 | tf_op jit(solution)/shard_map/all_to_all | solution.py:474
  321.9 114.7 %all-to-all-start.2 = ((bf16[128,8,4096]{2,1,0:T(8,128)(2,1)}), bf16[128,8,4096]{2,1,0:T(8,128)(2,1)}, u32[]{:S(2)}, u32[]{:S(2)}) async-start(bf16[128,8,4096]{2,1,0:T(8,128)(2,1)} %bitcast.99), calls=%async_computation.2 | async-start | bytes 16777216 | tf_op jit(solution)/shard_map/all_to_all | solution.py:474
  (23 other events, 919.6 us)

commit v5 on v4

--- a/solution.py
+++ b/solution.py
@@ -53,7 +53,7 @@
 
 
 def gather_line(part, shifts):
-    return jnp.stack([part] + [lax.ppermute(part, "exp", shifts(d)) for d in range(1, RING)])
+    return jnp.stack(gather_plane(part, shifts))
 
 
 def gather_plane(line, shifts):
@@ -442,8 +442,8 @@
 
     by_head = lambda a: a[0].reshape(tokens, seq_count, -1)
     heads = jnp.concatenate([by_head(queries), by_head(rotated_keys), by_head(projected_values)], axis=2)
-    heads = lax.all_to_all(heads.transpose(1, 0, 2), "seq", split_axis=0, concat_axis=0, tiled=True)
-    heads, upper, lower = lax.optimization_barrier((heads, upper, lower))
+    heads = heads.transpose(1, 0, 2)
+    heads = lax.all_to_all(heads, "seq", split_axis=0, concat_axis=0, tiled=True)
     upper, lower = gather_plane(upper, along_z), gather_plane(lower, along_x)
     heads = heads.reshape(seq_count * tokens, -1)
     q_width = width // seq_count

time: 448 us -> 458 us (1.022)
  waiting for transfers between devices: 143 us -> 149 us
    ppermute x6 -> x12, starting transfers between devices: 9.55 us -> 22.2 us  [gather_plane(): gathered.append(lax.ppermute(line, 'exp', shifts(d)))]
    ppermute x6 -> x12, waiting for transfers between devices: 23.8 us -> 34.9 us  [gather_plane(): gathered.append(lax.ppermute(line, 'exp', shifts(d)))]
    ppermute x6 -> x0, starting transfers between devices: 10.1 us -> none  [gather_line(): lax.ppermute(part, 'exp', shifts(d))]
    ppermute x6 -> x0, waiting for transfers between devices: 5.33 us -> none  [gather_line(): lax.ppermute(part, 'exp', shifts(d))]
  transfers between devices with their start and end apart: 23 -> 23, of which waited for: 14 -> 17; matrix products, arithmetic and copies ran while one was open for 8% -> 8% of each run, Pallas kernels for 7% -> 7%
where the time goes in v5:
time: 458 us; the launch traced here: 457 us
  waiting for transfers between devices  149 us (33%)
  blocking collectives  128 us (28%)
  Pallas kernels  72.8 us (16%)
  starting transfers between devices  60.2 us (13%)
  local copies, waits for them, and re-layouts  23.5 us (5%)
  matrix products  12.8 us (3%)
  other arithmetic  10 us (2%)
    all_to_all x1, blocking collectives, exchange(): lax.all_to_all(blocks, ('seq', 'exp'), split_axis=0, concat_axis=0, tiled...  128 us
    all_to_all x2, waiting for transfers between devices, exchange(): lax.all_to_all(blocks, ('seq', 'exp'), split_axis=0, concat_axis=0, tiled...  81.7 us
    pallas_call x2, Pallas kernels, run_expert(): pl.pallas_call(main_kernel if main else extra_kernel, grid=(2 * QUARTERS,...  39 us
    ppermute x12, waiting for transfers between devices, gather_plane(): gathered.append(lax.ppermute(line, 'exp', shifts(d)))  34.9 us
    ppermute x7, waiting for transfers between devices, layer(): sums[index] = lax.ppermute(sums[index], ('seq', 'exp'), around)  30.7 us
    ppermute x12, starting transfers between devices, gather_plane(): gathered.append(lax.ppermute(line, 'exp', shifts(d)))  22.2 us
    all_to_all x2, starting transfers between devices, exchange(): lax.all_to_all(blocks, ('seq', 'exp'), split_axis=0, concat_axis=0, tiled...  17.1 us
    ppermute x7, starting transfers between devices, layer(): sums[index] = lax.ppermute(sums[index], ('seq', 'exp'), around)  15.9 us
  transfers between devices with their start and end apart: 23, of which 17 were waited for; matrix products, arithmetic and copies ran while one was open for 8% of the time, Pallas kernels for 7%

profile of v5, /device:TPU:10, one launch (start us, length us, event | category | flops | bytes accessed | tf_op | source)
XLA Modules:
  0.0 456.8 jit_solution(2995881803984705890)
XLA Ops:
  6.0 4.9 %all-to-all-start = ((bf16[4,128,1280]{2,1,0:T(8,128)(2,1)}), bf16[4,128,1280]{2,1,0:T(8,128)(2,1)S(1)}, u32[]{:S(2)}, u32[]{:S(2)}) async-start(bf16[4,128,1280]{2,1,0:T(8,128)(2,1)} %maximum_bitcast_fusion), calls=%async_computation | async-start | bytes 2621440 | tf_op jit(solution)/shard_map/all_to_all | solution.py:446
  22.4 3.6 collective-permute-start.5
  28.8 7.5 %fusion.20 = (f32[8,512]{1,0:T(8,128)S(1)}, f32[8,512,512]{1,2,0:T(8,128)}) fusion(pred[512,512]{0,1:T(8,128)(4,1)S(1)} %fusion.9, bf16[512,8,128]{0,2,1:T(8,128)(2,1)} %bitcast.107, bf16[512,1280]{1,0:T(8,128)(2,1)S(1)} %bitcast.101), kind=kOutput, calls=%fused_computation.56 | convolution fusion | flops 545260032 | bytes 9846784 | tf_op jit(solution)/shard_map/sub | solution.py:37
  36.4 5.1 %fusion.6 = bf16[128,8,512]{2,0,1:T(8,128)(2,1)} fusion(f32[8,512,512]{1,2,0:T(8,128)} %get-tuple-element.37, f32[8,512]{1,0:T(8,128)S(1)} %get-tuple-element.36, bf16[512,1280]{1,0:T(8,128)(2,1)S(1)} %bitcast.102), kind=kOutput, calls=%fused_computation.10 | convolution fusion | flops 541589504 | bytes 9584640 | tf_op jit(solution)/shard_map/grj,jd->rgd/dot_general | solution.py:39
  43.1 4.1 collective-permute-start.9
  47.2 6.2 %collective-permute-done.9 = bf16[512,128]{1,0:T(8,128)(2,1)S(1)} collective-permute-done((bf16[512,128]{1,0:T(8,128)(2,1)S(1)}, bf16[512,128]{1,0:T(8,128)(2,1)S(1)}, u32[]{:S(2)}, u32[]{:S(2)}) %collective-permute-start.9) | collective-permute-done | bytes 131104 | tf_op jit(solution)/shard_map/ppermute | solution.py:62
  57.1 3.2 collective-permute-done.7
  68.0 7.3 %collective-permute-done.10.rest_5_ = bf16[4,512,128]{2,1,0:T(8,128)(2,1)} collective-permute-done((bf16[4,512,128]{2,1,0:T(8,128)(2,1)S(1)}, bf16[4,512,128]{2,1,0:T(8,128)(2,1)}, u32[]{:S(2)}, u32[]{:S(2)}) %collective-permute-start.10) | collective-permute-done | bytes 524320 | tf_op jit(solution)/shard_map/ppermute | solution.py:62
  78.3 8.3 %collective-permute-done.12.rest_7_ = bf16[4,512,128]{2,1,0:T(8,128)(2,1)} collective-permute-done((bf16[4,512,128]{2,1,0:T(8,128)(2,1)S(1)}, bf16[4,512,128]{2,1,0:T(8,128)(2,1)}, u32[]{:S(2)}, u32[]{:S(2)}) %collective-permute-start.12) | collective-permute-done | bytes 524320 | tf_op jit(solution)/shard_map/ppermute | solution.py:62
  86.7 11.5 %project.1 = (f32[128,2048]{1,0:T(8,128)}, bf16[128,2048]{1,0:T(8,128)(2,1)}, bf16[128,2048]{1,0:T(8,128)(2,1)}, bf16[128,2048]{1,0:T(8,128)(2,1)}, bf16[128,204...) custom-call(s32[4]{0:T(128)} %pad_add_fusion.place, ...), custom_call_target="tpu_custom_call" | custom-call | tf_op jit(solution)/shard_map/project/pallas_call | solution.py:111
  98.5 3.5 collective-permute-start.14
  104.6 8.8 %collective-permute-done.13.refs_1_ = bf16[128,2048]{1,0:T(8,128)(2,1)S(1)} collective-permute-done((bf16[128,2048]{1,0:T(8,128)(2,1)}, bf16[128,2048]{1,0:T(8,128)(2,1)S(1)}, u32[]{:S(2)}, u32[]{:S(2)}) %collective-permute-start.13) | collective-permute-done | bytes 524320 | tf_op jit(solution)/shard_map/ppermute | solution.py:467
  115.1 9.9 %collective-permute-start.19 = (bf16[128,2048]{1,0:T(8,128)(2,1)}, bf16[128,2048]{1,0:T(8,128)(2,1)}, u32[]{:S(2)}, u32[]{:S(2)}) collective-permute-start(bf16[128,2048]{1,0:T(8,128)(2,1)} %get-tuple-element.23), channel_id=1, source_target_pairs={{0,97},{1,96},{2,99},{3,98},{4,101},{5,100},{6,103},{7,102},{8,105... | collective-permute-start | bytes 1572872 | tf_op jit(solution)/shard_map/ppermute | solution.py:467
  127.0 5.7 %collective-permute-done.17.refs_5_ = bf16[128,2048]{1,0:T(8,128)(2,1)} collective-permute-done((bf16[128,2048]{1,0:T(8,128)(2,1)}, bf16[128,2048]{1,0:T(8,128)(2,1)}, u32[]{:S(2)}, u32[]{:S(2)}) %collective-permute-start.17) | collective-permute-done | bytes 524320 | tf_op jit(solution)/shard_map/ppermute | solution.py:467
  133.3 13.9 %collective-permute-done.19.refs_7_ = bf16[128,2048]{1,0:T(8,128)(2,1)} collective-permute-done((bf16[128,2048]{1,0:T(8,128)(2,1)}, bf16[128,2048]{1,0:T(8,128)(2,1)}, u32[]{:S(2)}, u32[]{:S(2)}) %collective-permute-start.19) | collective-permute-done | bytes 524320 | tf_op jit(solution)/shard_map/ppermute | solution.py:467
  148.5 8.4 %norm_pack.1 = (f32[128,4096]{1,0:T(8,128)S(1)}, bf16[1024,5120]{1,0:T(8,128)(2,1)S(1)}) custom-call(s32[4]{0:T(128)S(1)} %copy-done.9, f32[128,2048]{1,0:T(8,128)S(1)} %copy-done.6, bf16[128,2048]{1,0:T(8,128)(2,1)S(1)} %collective-permute-done.13.refs_1_, bf16[128,2048]{1,0:T(8,128)(2,1)S(1)} %collective-permute-done.14.refs_2_, ...), custom_call_target="tpu_custom_call" | custom-call | tf_op jit(solution)/shard_map/norm_pack/pallas_call | solution.py:173
  158.3 127.6 %all_to_all.20 = bf16[128,8,5120]{2,1,0:T(8,128)(2,1)S(1)} all-to-all(bf16[128,8,5120]{2,1,0:T(8,128)(2,1)S(1)} %bitcast.93), channel_id=1, replica_groups=mesh['seq'=4,'exp'=32] {'seq','exp'}, dimensions={0} | all-to-all | bytes 20971520 | tf_op jit(solution)/shard_map/all_to_all | solution.py:474
  285.9 10.5 %experts_extra.1.after = bf16[1024,1024]{1,0:T(8,128)(2,1)} custom-call(bf16[1024,5120]{1,0:T(8,128)(2,1)S(1)} %bitcast.83, bf16[4096,1536]{1,0:T(8,128)(2,1)S(1)} %bitcast.88, bf16[768,4096]{1,0:T(8,128)(2,1)S(1)} %bitcast.92), custom_call_target="tpu_custom_call" | custom-call | tf_op jit(solution)/shard_map/experts_extra/pallas_call | solution.py:290
  296.4 6.9 %all-to-all-start.3 = ((bf16[128,8,1024]{2,1,0:T(8,128)(2,1)}), bf16[128,8,1024]{2,1,0:T(8,128)(2,1)S(1)}, u32[]{:S(2)}, u32[]{:S(2)}) async-start(bf16[128,8,1024]{2,1,0:T(8,128)(2,1)} %bitcast.34), calls=%async_computation.3 | async-start | bytes 4194304 | tf_op jit(solution)/shard_map/all_to_all | solution.py:474
  303.3 28.6 %experts_main.1 = bf16[1024,4096]{1,0:T(8,128)(2,1)} custom-call(bf16[1024,1024]{1,0:T(8,128)(2,1)} %experts_extra.1.after, bf16[1024,5120]{1,0:T(8,128)(2,1)} %bitcast.84, bf16[4096,1536]{1,0:T(8,128)(2,1)} %bitcast.85, bf16[768,4096]{1,0:T(8,128)(2,1)} %bitcast.89), custom_call_target="tpu_custom_call" | custom-call | tf_op jit(solution)/shard_map/experts_main/pallas_call | solution.py:290
  331.9 10.2 %all-to-all-start.2 = ((bf16[128,8,4096]{2,1,0:T(8,128)(2,1)}), bf16[128,8,4096]{2,1,0:T(8,128)(2,1)}, u32[]{:S(2)}, u32[]{:S(2)}) async-start(bf16[128,8,4096]{2,1,0:T(8,128)(2,1)} %bitcast.99), calls=%async_computation.2 | async-start | bytes 16777216 | tf_op jit(solution)/shard_map/all_to_all | solution.py:474
  359.3 3.7 combine_extra.1
  365.0 81.7 %all-to-all-done.2 = bf16[128,8,4096]{2,1,0:T(8,128)(2,1)} async-done(((bf16[128,8,4096]{2,1,0:T(8,128)(2,1)}), bf16[128,8,4096]{2,1,0:T(8,128)(2,1)}, u32[]{:S(2)}, u32[]{:S(2)}) %all-to-all-start.2) | async-done | bytes 8388640 | tf_op jit(solution)/shard_map/all_to_all | solution.py:474
  446.7 10.1 %combine_main.1 = (bf16[128,4096]{1,0:T(8,128)(2,1)}, f32[8,128]{1,0:T(8,128)}) custom-call(bf16[1024,4096]{1,0:T(8,128)(2,1)} %bitcast.33.main, f32[128,4096]{1,0:T(8,128)} %copy-done.4, bf16[128,4096]{1,0:T(8,128)(2,1)} %bitcast.95, bf16[256,1024]{1,0:T(8,128)(2,1)} %pad_maximum_fusion.2.gates, s32[128,8]{1,0:T(8,128)} %get-tuple-element.34.keys, ...), custom_call_target="tpu_custom_call" | custom-call | tf_op jit(solution)/shard_map/combine_main/pallas_call | solution.py:369
  (131 shorter events, 64.3 us)
Async XLA Ops:
  6.0 21.4 %all-to-all-start = ((bf16[4,128,1280]{2,1,0:T(8,128)(2,1)}), bf16[4,128,1280]{2,1,0:T(8,128)(2,1)S(1)}, u32[]{:S(2)}, u32[]{:S(2)}) async-start(bf16[4,128,1280]{2,1,0:T(8,128)(2,1)} %maximum_bitcast_fusion), calls=%async_computation | async-start | bytes 2621440 | tf_op jit(solution)/shard_map/all_to_all | solution.py:446
  11.0 6.1 %collective-permute-start.3 = (bf16[512,128]{1,0:T(8,128)(2,1)S(1)}, bf16[512,128]{1,0:T(8,128)(2,1)S(1)}, u32[]{:S(2)}, u32[]{:S(2)}) collective-permute-start(bf16[512,128]{1,0:T(8,128)(2,1)S(1)} %get-tuple-element.33), channel_id=1, source_target_pairs={{0,6},{1,7},{2,0},{3,1},{4,2},{5,3},{6,4},{7,5},{8,14},{9,15},{10,... | collective-permute-start | bytes 393224 | tf_op jit(solution)/shard_map/ppermute | solution.py:62
  11.6 7.9 %collective-permute-start.2 = (bf16[512,128]{1,0:T(8,128)(2,1)S(1)}, bf16[512,128]{1,0:T(8,128)(2,1)S(1)}, u32[]{:S(2)}, u32[]{:S(2)}) collective-permute-start(bf16[512,128]{1,0:T(8,128)(2,1)S(1)} %get-tuple-element.33), channel_id=1, source_target_pairs={{0,4},{1,5},{2,6},{3,7},{4,0},{5,1},{6,2},{7,3},{8,12},{9,13},{10,... | collective-permute-start | bytes 393224 | tf_op jit(solution)/shard_map/ppermute | solution.py:62
  14.0 6.3 %collective-permute-start.1 = (bf16[512,128]{1,0:T(8,128)(2,1)S(1)}, bf16[512,128]{1,0:T(8,128)(2,1)S(1)}, u32[]{:S(2)}, u32[]{:S(2)}) collective-permute-start(bf16[512,128]{1,0:T(8,128)(2,1)S(1)} %get-tuple-element.33), channel_id=1, source_target_pairs={{0,2},{1,3},{2,4},{3,5},{4,6},{5,7},{6,0},{7,1},{8,10},{9,11},{10,... | collective-permute-start | bytes 393224 | tf_op jit(solution)/shard_map/ppermute | solution.py:62
  20.4 41.5 %collective-permute-start.4 = (bf16[4,512,128]{2,1,0:T(8,128)(2,1)S(1)}, bf16[4,512,128]{2,1,0:T(8,128)(2,1)}, u32[]{:S(2)}, u32[]{:S(2)}) collective-permute-start(bf16[4,512,128]{2,1,0:T(8,128)(2,1)S(1)} %pad_maximum_fusion.rest_0_), channel_id=1, source_target_pairs={{0,8},{1,9},{2,10},{3,11},{4,12},{5,13},{6,14},{7,15},{8,16},{9,17... | collective-permute-start | bytes 1572872 | tf_op jit(solution)/shard_map/ppermute | solution.py:62
  22.4 40.6 %collective-permute-start.5 = (bf16[4,512,128]{2,1,0:T(8,128)(2,1)S(1)}, bf16[4,512,128]{2,1,0:T(8,128)(2,1)}, u32[]{:S(2)}, u32[]{:S(2)}) collective-permute-start(bf16[4,512,128]{2,1,0:T(8,128)(2,1)S(1)} %pad_maximum_fusion.rest_0_), channel_id=1, source_target_pairs={{0,16},{1,17},{2,18},{3,19},{4,20},{5,21},{6,22},{7,23},{8,24},{9,... | collective-permute-start | bytes 1572872 | tf_op jit(solution)/shard_map/ppermute | solution.py:62
  43.0 43.7 %collective-permute-start = (bf16[512,1024]{1,0:T(8,128)(2,1)S(1)}, bf16[512,1024]{1,0:T(8,128)(2,1)}, u32[]{:S(2)}, u32[]{:S(2)}) collective-permute-start(bf16[512,1024]{1,0:T(8,128)(2,1)S(1)} %copy.63.mine), channel_id=1, source_target_pairs={{0,1},{1,0},{2,3},{3,2},{4,5},{5,4},{6,7},{7,6},{8,9},{9,8},{10,11... | collective-permute-start | bytes 3145736 | tf_op jit(solution)/shard_map/ppermute | solution.py:456
  43.1 10.3 %collective-permute-start.9 = (bf16[512,128]{1,0:T(8,128)(2,1)S(1)}, bf16[512,128]{1,0:T(8,128)(2,1)S(1)}, u32[]{:S(2)}, u32[]{:S(2)}) collective-permute-start(bf16[512,128]{1,0:T(8,128)(2,1)S(1)} %get-tuple-element.32), channel_id=1, source_target_pairs={{0,24},{1,25},{2,26},{3,27},{4,28},{5,29},{6,30},{7,31},{8,0},{9,1... | collective-permute-start | bytes 393224 | tf_op jit(solution)/shard_map/ppermute | solution.py:62
  47.2 7.1 %collective-permute-start.8 = (bf16[512,128]{1,0:T(8,128)(2,1)S(1)}, bf16[512,128]{1,0:T(8,128)(2,1)S(1)}, u32[]{:S(2)}, u32[]{:S(2)}) collective-permute-start(bf16[512,128]{1,0:T(8,128)(2,1)S(1)} %get-tuple-element.32), channel_id=1, source_target_pairs={{0,16},{1,17},{2,18},{3,19},{4,20},{5,21},{6,22},{7,23},{8,24},{9,... | collective-permute-start | bytes 393224 | tf_op jit(solution)/shard_map/ppermute | solution.py:62
  53.3 6.9 %collective-permute-start.7 = (bf16[512,128]{1,0:T(8,128)(2,1)S(1)}, bf16[512,128]{1,0:T(8,128)(2,1)S(1)}, u32[]{:S(2)}, u32[]{:S(2)}) collective-permute-start(bf16[512,128]{1,0:T(8,128)(2,1)S(1)} %get-tuple-element.32), channel_id=1, source_target_pairs={{0,8},{1,9},{2,10},{3,11},{4,12},{5,13},{6,14},{7,15},{8,16},{9,17... | collective-permute-start | bytes 393224 | tf_op jit(solution)/shard_map/ppermute | solution.py:62
  54.2 13.8 %collective-permute-start.6 = (bf16[4,512,128]{2,1,0:T(8,128)(2,1)S(1)}, bf16[4,512,128]{2,1,0:T(8,128)(2,1)}, u32[]{:S(2)}, u32[]{:S(2)}) collective-permute-start(bf16[4,512,128]{2,1,0:T(8,128)(2,1)S(1)} %pad_maximum_fusion.rest_0_), channel_id=1, source_target_pairs={{0,24},{1,25},{2,26},{3,27},{4,28},{5,29},{6,30},{7,31},{8,0},{9,1... | collective-permute-start | bytes 1572872 | tf_op jit(solution)/shard_map/ppermute | solution.py:62
  60.4 15.0 %collective-permute-start.10 = (bf16[4,512,128]{2,1,0:T(8,128)(2,1)S(1)}, bf16[4,512,128]{2,1,0:T(8,128)(2,1)}, u32[]{:S(2)}, u32[]{:S(2)}) collective-permute-start(bf16[4,512,128]{2,1,0:T(8,128)(2,1)S(1)} %pad_maximum_fusion.1.rest_4_), channel_id=1, source_target_pairs={{0,2},{1,3},{2,4},{3,5},{4,6},{5,7},{6,0},{7,1},{8,10},{9,11},{10,... | collective-permute-start | bytes 1572872 | tf_op jit(solution)/shard_map/ppermute | solution.py:62
  61.9 16.4 %collective-permute-start.11 = (bf16[4,512,128]{2,1,0:T(8,128)(2,1)S(1)}, bf16[4,512,128]{2,1,0:T(8,128)(2,1)}, u32[]{:S(2)}, u32[]{:S(2)}) collective-permute-start(bf16[4,512,128]{2,1,0:T(8,128)(2,1)S(1)} %pad_maximum_fusion.1.rest_4_), channel_id=1, source_target_pairs={{0,4},{1,5},{2,6},{3,7},{4,0},{5,1},{6,2},{7,3},{8,12},{9,13},{10,... | collective-permute-start | bytes 1572872 | tf_op jit(solution)/shard_map/ppermute | solution.py:62
  63.0 23.6 %collective-permute-start.12 = (bf16[4,512,128]{2,1,0:T(8,128)(2,1)S(1)}, bf16[4,512,128]{2,1,0:T(8,128)(2,1)}, u32[]{:S(2)}, u32[]{:S(2)}) collective-permute-start(bf16[4,512,128]{2,1,0:T(8,128)(2,1)S(1)} %pad_maximum_fusion.1.rest_4_), channel_id=1, source_target_pairs={{0,6},{1,7},{2,0},{3,1},{4,2},{5,3},{6,4},{7,5},{8,14},{9,15},{10,... | collective-permute-start | bytes 1572872 | tf_op jit(solution)/shard_map/ppermute | solution.py:62
  98.2 15.3 %collective-permute-start.13 = (bf16[128,2048]{1,0:T(8,128)(2,1)}, bf16[128,2048]{1,0:T(8,128)(2,1)S(1)}, u32[]{:S(2)}, u32[]{:S(2)}) collective-permute-start(bf16[128,2048]{1,0:T(8,128)(2,1)} %get-tuple-element.17), channel_id=1, source_target_pairs={{0,32},{1,33},{2,34},{3,35},{4,36},{5,37},{6,38},{7,39},{8,40},{9,... | collective-permute-start | bytes 1572872 | tf_op jit(solution)/shard_map/ppermute | solution.py:467
  98.5 16.6 %collective-permute-start.14 = (bf16[128,2048]{1,0:T(8,128)(2,1)}, bf16[128,2048]{1,0:T(8,128)(2,1)S(1)}, u32[]{:S(2)}, u32[]{:S(2)}) collective-permute-start(bf16[128,2048]{1,0:T(8,128)(2,1)} %get-tuple-element.18), channel_id=1, source_target_pairs={{0,64},{1,65},{2,66},{3,67},{4,68},{5,69},{6,70},{7,71},{8,72},{9,... | collective-permute-start | bytes 1572872 | tf_op jit(solution)/shard_map/ppermute | solution.py:467
  102.4 24.6 %collective-permute-start.15 = (bf16[128,2048]{1,0:T(8,128)(2,1)}, bf16[128,2048]{1,0:T(8,128)(2,1)S(1)}, u32[]{:S(2)}, u32[]{:S(2)}) collective-permute-start(bf16[128,2048]{1,0:T(8,128)(2,1)} %get-tuple-element.19), channel_id=1, source_target_pairs={{0,96},{1,97},{2,98},{3,99},{4,100},{5,101},{6,102},{7,103},{8,104... | collective-permute-start | bytes 1572872 | tf_op jit(solution)/shard_map/ppermute | solution.py:467
  103.0 24.1 %collective-permute-start.16 = (bf16[128,2048]{1,0:T(8,128)(2,1)}, bf16[128,2048]{1,0:T(8,128)(2,1)S(1)}, u32[]{:S(2)}, u32[]{:S(2)}) collective-permute-start(bf16[128,2048]{1,0:T(8,128)(2,1)} %get-tuple-element.20), channel_id=1, source_target_pairs={{0,1},{1,0},{2,3},{3,2},{4,5},{5,4},{6,7},{7,6},{8,9},{9,8},{10,11... | collective-permute-start | bytes 1572872 | tf_op jit(solution)/shard_map/ppermute | solution.py:467
  103.0 29.8 %collective-permute-start.17 = (bf16[128,2048]{1,0:T(8,128)(2,1)}, bf16[128,2048]{1,0:T(8,128)(2,1)}, u32[]{:S(2)}, u32[]{:S(2)}) collective-permute-start(bf16[128,2048]{1,0:T(8,128)(2,1)} %get-tuple-element.21), channel_id=1, source_target_pairs={{0,33},{1,32},{2,35},{3,34},{4,37},{5,36},{6,39},{7,38},{8,41},{9,... | collective-permute-start | bytes 1572872 | tf_op jit(solution)/shard_map/ppermute | solution.py:467
  113.4 19.9 %collective-permute-start.18 = (bf16[128,2048]{1,0:T(8,128)(2,1)}, bf16[128,2048]{1,0:T(8,128)(2,1)}, u32[]{:S(2)}, u32[]{:S(2)}) collective-permute-start(bf16[128,2048]{1,0:T(8,128)(2,1)} %get-tuple-element.22), channel_id=1, source_target_pairs={{0,65},{1,64},{2,67},{3,66},{4,69},{5,68},{6,71},{7,70},{8,73},{9,... | collective-permute-start | bytes 1572872 | tf_op jit(solution)/shard_map/ppermute | solution.py:467
  115.1 32.2 %collective-permute-start.19 = (bf16[128,2048]{1,0:T(8,128)(2,1)}, bf16[128,2048]{1,0:T(8,128)(2,1)}, u32[]{:S(2)}, u32[]{:S(2)}) collective-permute-start(bf16[128,2048]{1,0:T(8,128)(2,1)} %get-tuple-element.23), channel_id=1, source_target_pairs={{0,97},{1,96},{2,99},{3,98},{4,101},{5,100},{6,103},{7,102},{8,105... | collective-permute-start | bytes 1572872 | tf_op jit(solution)/shard_map/ppermute | solution.py:467
  148.5 137.4 %slice-start = ((s8[12582912]{0:T(1024)(128)(4,1)}), s8[4194304]{0:T(1024)(128)(4,1)S(1)}, s32[]{:S(2)}) async-start(s8[12582912]{0:T(1024)(128)(4,1)} %bitcast.86), calls=%async_computation.4 | async-start | bytes 8388608
  296.4 35.5 %all-to-all-start.3 = ((bf16[128,8,1024]{2,1,0:T(8,128)(2,1)}), bf16[128,8,1024]{2,1,0:T(8,128)(2,1)S(1)}, u32[]{:S(2)}, u32[]{:S(2)}) async-start(bf16[128,8,1024]{2,1,0:T(8,128)(2,1)} %bitcast.34), calls=%async_computation.3 | async-start | bytes 4194304 | tf_op jit(solution)/shard_map/all_to_all | solution.py:474
  331.9 114.7 %all-to-all-start.2 = ((bf16[128,8,4096]{2,1,0:T(8,128)(2,1)}), bf16[128,8,4096]{2,1,0:T(8,128)(2,1)}, u32[]{:S(2)}, u32[]{:S(2)}) async-start(bf16[128,8,4096]{2,1,0:T(8,128)(2,1)} %bitcast.99), calls=%async_computation.2 | async-start | bytes 16777216 | tf_op jit(solution)/shard_map/all_to_all | solution.py:474
  (23 other events, 952.7 us)
